TPU v7x, 128 devices: a whole 4x4x4 slice. The times are simulated.
128 devices in a mesh: row: 16 (over x_hi, y, core), proto: 8 (over z, x_lo).
Axes of the slice: x: 4 (x_hi: 2, x_lo: 2; x = x_hi * 2 + x_lo), y: 4, z: 4, core: 2. Of those that a mesh axis runs over, the one named last changes fastest.
Arguments:
- tokens: bfloat16 [8192, 4096], P('row'), may hold values from -6 to 6
- w_in: bfloat16 [4096, 8192], P('row', 'proto'), may hold values from -0.09375 to 0.09375
- w_out: bfloat16 [8192, 384], P('proto'), may hold values from -0.0625 to 0.0625
- teacher_z: bfloat16 [8192, 384], P(('row', 'proto')), may hold values from -6 to 6
- proto_student: bfloat16 [384, 49152], P(None, 'proto'), may hold values from -48 to 48
- proto_teacher: bfloat16 [384, 49152], P(None, 'proto'), may hold values from -48 to 48
- center: float32 [49152], P('proto'), may hold values from -0.6 to 0.6
- image_of: int32 [8192], P('row'), may hold values from 0 to 63
Outputs:
- loss: float32 [], replicated
- w_in_grad: float32 [4096, 8192], P('row', 'proto')
- w_out_grad: float32 [8192, 384], P('proto')
- proto_grad: float32 [384, 49152], P('row', 'proto')
All inputs are finite; a program needn't handle non-finite values.
Results may differ from a plain program's by a relative error of at most 0.015.
Values may be sent and summed in bfloat16 or wider, within the bound.
A program may use at most 128 MiB of HBM per device.

v0:
```python
import jax
import jax.numpy as jnp
from jax import lax
from jax.sharding import PartitionSpec as P

tau_teacher = 0.07
tau_student = 0.1
loss_scale = 1048576.0
norm_eps = 1e-06


def gelu_parts(values):
    cumul = 0.5 * (1.0 + jax.scipy.special.erf(values * 0.7071067811865476))
    density = jnp.exp(-0.5 * values * values) * 0.3989422804014327
    return (values * cumul, cumul + values * density)


def inner(left, right):
    return lax.dot_general(
        left, right, (((0,), (0,)), ((), ())), preferred_element_type=jnp.float32
    )


def outer_last(left, right):
    return lax.dot_general(
        left, right, (((1,), (1,)), ((), ())), preferred_element_type=jnp.float32
    )


def normalize(values):
    recip = lax.rsqrt(jnp.sum(values * values, axis=1, keepdims=True) + norm_eps)
    return (recip, values * recip)


def teacher_norm(teacher_z):
    teach = teacher_z.astype(jnp.float32)
    return (teach * lax.rsqrt(jnp.sum(teach * teach, axis=1, keepdims=True) + norm_eps)).astype(
        jnp.bfloat16
    )


def back_norm(dnorm, recip, unit):
    return (recip * (dnorm - unit * jnp.sum(unit * dnorm, axis=1, keepdims=True))).astype(
        jnp.bfloat16
    )


def on_device(tokens, w_in, w_out, teacher_z, proto_student, proto_teacher, center, image_of):
    row_count = tokens.shape[0]
    images = row_count * lax.axis_size("row") // 128
    onehot = (image_of[:, None] == jnp.arange(images, dtype=jnp.int32)[None, :]).astype(jnp.float32)
    counts = lax.psum(jnp.sum(onehot, axis=0), "row")
    weight = 1.0 / (images * jnp.sum(onehot * counts[None, :], axis=1))
    pre = jnp.dot(
        tokens, lax.all_gather(w_in, "row", axis=0, tiled=True), preferred_element_type=jnp.float32
    )
    act, slope = gelu_parts(pre)
    hidden = act.astype(jnp.bfloat16)
    partial_value = jnp.dot(hidden, w_out, preferred_element_type=jnp.float32)
    bott = lax.psum(partial_value, "proto")
    recip, unit = normalize(bott)
    student_n = unit.astype(jnp.bfloat16)
    teacher_n = lax.all_gather(teacher_norm(teacher_z), "proto", axis=0, tiled=True)
    logit_t = (
        jnp.dot(teacher_n, proto_teacher, preferred_element_type=jnp.float32) - center[None, :]
    ) / tau_teacher
    logit_s = jnp.dot(student_n, proto_student, preferred_element_type=jnp.float32) / tau_student
    local_t = jnp.max(logit_t, axis=1)
    local_s = jnp.max(logit_s, axis=1)
    top_t, top_s = lax.pmax((local_t, local_s), "proto")
    exp_t = jnp.exp(logit_t - top_t[:, None])
    exp_s = jnp.exp(logit_s - top_s[:, None])
    total_t, total_s = lax.psum((jnp.sum(exp_t, axis=1), jnp.sum(exp_s, axis=1)), "proto")
    prob_t = exp_t / total_t[:, None]
    prob_s = exp_s / total_s[:, None]
    logp_s = logit_s - top_s[:, None] - jnp.log(total_s)[:, None]
    cross = -jnp.sum(prob_t * logp_s, axis=1)
    loss = lax.psum(jnp.sum(weight * cross), ("row", "proto"))
    grad_s = (loss_scale * weight[:, None] * (prob_s - prob_t) / tau_student).astype(jnp.bfloat16)
    proto_grad = lax.psum_scatter(
        inner(student_n, grad_s).astype(jnp.bfloat16), "row", scatter_dimension=0, tiled=True
    ).astype(jnp.float32)
    dnorm_part = outer_last(grad_s, proto_student)
    dnorm = lax.psum(dnorm_part, "proto")
    dbott = back_norm(dnorm, recip, unit)
    w_out_grad = lax.psum(inner(hidden, dbott).astype(jnp.bfloat16), "row").astype(jnp.float32)
    dpre = (outer_last(dbott, w_out) * slope).astype(jnp.bfloat16)
    w_in_grad = lax.psum_scatter(
        inner(tokens, dpre).astype(jnp.bfloat16), "row", scatter_dimension=0, tiled=True
    ).astype(jnp.float32)
    return (loss, w_in_grad, w_out_grad, proto_grad)


def solution(mesh):
    return jax.shard_map(
        on_device,
        mesh=mesh,
        in_specs=(
            P("row", None),
            P("row", "proto"),
            P("proto", None),
            P(("row", "proto"), None),
            P(None, "proto"),
            P(None, "proto"),
            P("proto"),
            P("row"),
        ),
        out_specs=(P(), P("row", "proto"), P("proto", None), P("row", "proto")),
        check_vma=False,
    )
```

profile of v0, /device:TPU:1, one launch (start us, length us, event | category | flops | bytes accessed | tf_op | source)
XLA Modules:
  0.0 675.2 jit_solution(12270464372114535581)
XLA Ops:
  8.8 34.7 %psum.49 = f32[64]{0:T(128)S(1)} all-reduce(f32[64]{0:T(128)S(1)} %convert_reduce_fusion), channel_id=1, replica_groups=mesh['row'=16,'proto'=8] {'row'}, use_global_device_ids=true, to_apply=%region_1.0 | all-reduce | flops 64 | bytes 512 | tf_op jit(solution)/shard_map/psum | solution.py:52
  46.1 40.6 %all-gather.2.cloned.1.call-done = bf16[4096,1024]{1,0:T(8,128)(2,1)} async-done(((bf16[256,1024]{1,0:T(8,128)(2,1)}), bf16[4096,1024]{1,0:T(8,128)(2,1)}) %all-gather.2.cloned.1.call-update) | async-done | bytes 8388624 | tf_op jit(solution)/shard_map/all_gather | solution.py:55
  86.7 10.6 %multiply_convert_fusion.1 = (bf16[512,1024]{1,0:T(8,128)(2,1)S(1)}, f32[512,1024]{1,0:T(8,128)}) fusion(bf16[512,4096]{1,0:T(8,128)(2,1)} %param.8, bf16[4096,1024]{1,0:T(8,128)(2,1)} %all-gather.2.cloned.1.call-done), kind=kOutput, calls=%fused_computation.19 | convolution fusion | flops 4297588736 | bytes 15728640 | tf_op jit(solution)/shard_map/dot_general | solution.py:54
  99.0 25.3 %all_gather.6 = bf16[512,384]{1,0:T(8,128)(2,1)S(1)} all-gather(bf16[64,384]{1,0:T(8,128)(2,1)S(1)} %fusion.10), channel_id=1, replica_groups=mesh['row'=16,'proto'=8] {'proto'}, dimensions={0}, use_global_device_ids=true | all-gather | bytes 442368 | tf_op jit(solution)/shard_map/all_gather | solution.py:63
  124.3 9.0 %fusion = (f32[512]{0:T(512)S(1)}, f32[512,6144]{1,0:T(8,128)}) fusion(f32[6144]{0:T(1024)S(1)} %copy-done.3, bf16[512,384]{1,0:T(8,128)(2,1)S(1)} %all_gather.6, bf16[384,6144]{1,0:T(8,128)(2,1)} %param.13), kind=kOutput, calls=%fused_computation.7 | convolution fusion | flops 2425355776 | bytes 17721344 | tf_op jit(solution)/shard_map/dot_general | solution.py:65
  133.3 38.4 %all-reduce.6.cloned.1.call-done = f32[512,384]{1,0:T(8,128)} async-done(((f32[512,384]{1,0:T(8,128)}), f32[512,384]{1,0:T(8,128)}) %all-reduce.6.cloned.1.call-update) | async-done | bytes 786448 | tf_op jit(solution)/shard_map/psum | solution.py:60
  172.9 10.7 %multiply_reduce_fusion.1 = (f32[512]{0:T(512)S(1)}, f32[512,6144]{1,0:T(8,128)}) fusion(bf16[384,6144]{1,0:T(8,128)(2,1)} %param.12, f32[512,384]{1,0:T(8,128)} %all-reduce.6.cloned.1.call-done, f32[512]{0:T(512)S(1)} %add_rsqrt_fusion), kind=kOutput, calls=%fused_computation.6 | convolution fusion | flops 2422603264 | bytes 18092032 | tf_op jit(solution)/shard_map/dot_general | solution.py:67
  183.6 14.2 %all-reduce.1 = (f32[512]{0:T(512)S(1)}, f32[512]{0:T(512)S(1)}) all-reduce(f32[512]{0:T(512)S(1)} %get-tuple-element.20, f32[512]{0:T(512)S(1)} %get-tuple-element.22), channel_id=1, replica_groups=mesh['row'=16,'proto'=8] {'proto'}, use_global_device_ids=true, to_apply=%region_11.0 | all-reduce | flops 1024 | bytes 8192 | tf_op jit(solution)/shard_map/pmax | solution.py:70
  197.8 10.3 %exponential_reduce_fusion = (f32[512]{0:T(512)S(1)}, f32[512]{0:T(512)S(1)}) fusion(f32[512,6144]{1,0:T(8,128)} %get-tuple-element.21, f32[512]{0:T(512)S(1)} %get-tuple-element.14, f32[512]{0:T(512)S(1)} %get-tuple-element.15, f32[512,6144]{1,0:T(8,128)} %get-tuple-element.23, f32[6144]{0:T(1024)S(1)} %copy-done.3), kind=kLoop, calls=%fused_computation.4 | loop fusion | flops 22019072 | bytes 25198592 | tf_op jit(solution)/shard_map/reduce_sum | solution.py:73
  208.1 12.7 %all-reduce = (f32[512]{0:T(512)S(1)}, f32[512]{0:T(512)S(1)}) all-reduce(f32[512]{0:T(512)S(1)} %get-tuple-element.24, f32[512]{0:T(512)S(1)} %get-tuple-element.25), channel_id=1, replica_groups=mesh['row'=16,'proto'=8] {'proto'}, use_global_device_ids=true, to_apply=%region_13.0 | all-reduce | flops 1024 | bytes 8192 | tf_op jit(solution)/shard_map/psum | solution.py:73
  220.8 12.0 %multiply_convert_fusion = (bf16[512,6144]{1,0:T(8,128)(2,1)S(1)}, f32[512]{0:T(512)S(1)}) fusion(f32[512,6144]{1,0:T(8,128)} %get-tuple-element.21, f32[512]{0:T(512)S(1)} %get-tuple-element.12, f32[512]{0:T(512)S(1)} %broadcast_multiply_fusion, f32[512]{0:T(512)S(1)} %get-tuple-element.14, f32[512]{0:T(512)S(1)} %get-tuple-element.13, ...), kind=kLoop, calls=%fused_computation | loop fusion | flops 44039680 | bytes 31496192 | tf_op jit(solution)/shard_map/convert_element_type | solution.py:79
  232.8 2.7 copy-done.1
  235.5 6.7 fusion.15
  242.3 84.1 %all-reduce.8.cloned.1.call-done = f32[512,384]{1,0:T(8,128)} async-done(((f32[512,384]{1,0:T(8,128)}), f32[512,384]{1,0:T(8,128)}) %all-reduce.8.cloned.1.call-update) | async-done | bytes 786448 | tf_op jit(solution)/shard_map/psum | solution.py:84
  329.1 1.7 convolution_convert_fusion.1
  330.8 7.7 %convolution_convert_fusion = bf16[384,6144]{1,0:T(8,128)(2,1)} fusion(bf16[512,6144]{1,0:T(8,128)(2,1)} %copy-done.1, f32[512,384]{1,0:T(8,128)S(1)} %copy-done.2, f32[512]{0:T(512)S(1)} %add_rsqrt_fusion), kind=kOutput, calls=%fused_computation.10 | convolution fusion | flops 2418671616 | bytes 11798528 | tf_op jit(solution)/shard_map/dot_general | solution.py:19
  338.6 10.3 %convert_bitcast_fusion = bf16[4096,1024]{0,1:T(8,128)(2,1)} fusion(bf16[512,4096]{1,0:T(8,128)(2,1)} %param.8, f32[512,1024]{1,0:T(8,128)} %get-tuple-element.19, bf16[512,384]{1,0:T(8,128)(2,1)S(1)} %multiply_convert_fusion.2, bf16[1024,384]{1,0:T(8,128)(2,1)S(1)} %copy-done), kind=kOutput, calls=%fused_computation.11 | convolution fusion | flops 4707057664 | bytes 15859712 | tf_op jit(solution)/shard_map/dot_general | solution.py:19
  349.6 67.4 %psum.53 = f32[]{:T(128)} all-reduce(f32[]{:T(128)} %multiply_reduce_fusion.4), channel_id=1, replica_groups=mesh['row'=16,'proto'=8] {'row','proto'}, use_global_device_ids=true, to_apply=%region_16.0 | all-reduce | flops 1 | bytes 8 | tf_op jit(solution)/shard_map/psum | solution.py:78
  417.0 57.7 %all-reduce.10.cloned.1.call-done = bf16[1024,384]{1,0:T(8,128)(2,1)} async-done(((bf16[1024,384]{1,0:T(8,128)(2,1)}), bf16[1024,384]{1,0:T(8,128)(2,1)}) %all-reduce.10.cloned.1.call-update) | async-done | bytes 786448 | tf_op jit(solution)/shard_map/psum | solution.py:86
  474.6 2.4 convert_element_type.57
  477.0 84.1 %reduce-scatter.5.cloned.1.call-done = bf16[24,6144]{1,0:T(8,128)(2,1)} async-done(((bf16[384,6144]{1,0:T(8,128)(2,1)}), bf16[24,6144]{1,0:T(8,128)(2,1)}) %reduce-scatter.5.cloned.1.call-update) | async-done | bytes 294928 | tf_op jit(solution)/shard_map/reduce_scatter | solution.py:80
  561.1 1.8 convert_element_type.59
  562.9 103.2 %reduce-scatter.3.cloned.1.call-done = bf16[256,1024]{0,1:T(8,128)(2,1)} async-done(((bf16[4096,1024]{0,1:T(8,128)(2,1)}), bf16[256,1024]{0,1:T(8,128)(2,1)}) %reduce-scatter.3.cloned.1.call-update) | async-done | bytes 524304 | tf_op jit(solution)/shard_map/reduce_scatter | solution.py:88
  666.2 2.2 copy.13
  (32 shorter events, 10.6 us)
Async XLA Ops:
  7.2 90.1 %copy-start = (bf16[1024,384]{1,0:T(8,128)(2,1)S(1)}, bf16[1024,384]{1,0:T(8,128)(2,1)}, u32[]{:S(2)}) copy-start(bf16[1024,384]{1,0:T(8,128)(2,1)} %param.10) | copy-start | bytes 2359300
  7.2 79.5 %all-gather.2.cloned.1.call-start = ((), (), s32[]{:S(2)}) async-start(), calls=%async_computation.2 | async-start | bytes 8912896 | tf_op jit(solution)/shard_map/all_gather | solution.py:55
  7.9 163.7 %all-reduce.6.cloned.1.call-start = ((), (), s32[]{:S(2)}) async-start(), calls=%async_computation.3 | async-start | bytes 1572864 | tf_op jit(solution)/shard_map/psum | solution.py:60
  46.1 78.2 %copy-start.3 = (f32[6144]{0:T(1024)S(1)}, f32[6144]{0:T(1024)}, u32[]{:S(2)}) copy-start(f32[6144]{0:T(1024)} %param.14) | copy-start | bytes 73732
  98.9 227.5 %all-reduce.8.cloned.1.call-start = ((), (), s32[]{:S(2)}) async-start(), calls=%async_computation.4 | async-start | bytes 1572864 | tf_op jit(solution)/shard_map/psum | solution.py:84
  232.8 2.7 copy-start.1
  235.5 90.9 %copy-start.2 = (f32[512,384]{1,0:T(8,128)S(1)}, f32[512,384]{1,0:T(8,128)}, u32[]{:S(2)}) copy-start(f32[512,384]{1,0:T(8,128)} %all-reduce.6.cloned.1.call-done) | copy-start | bytes 2359300
  242.2 232.4 %all-reduce.10.cloned.1.call-start = ((), (), s32[]{:S(2)}) async-start(), calls=%async_computation.6 | async-start | bytes 1572864 | tf_op jit(solution)/shard_map/psum | solution.py:86
  330.8 230.3 %reduce-scatter.5.cloned.1.call-start = ((), (), s32[]{:S(2)}) async-start(), calls=%async_computation.7 | async-start | bytes 5013504 | tf_op jit(solution)/shard_map/reduce_scatter | solution.py:80
  338.5 327.6 %reduce-scatter.3.cloned.1.call-start = ((), (), s32[]{:S(2)}) async-start(), calls=%async_computation.5 | async-start | bytes 8912896 | tf_op jit(solution)/shard_map/reduce_scatter | solution.py:88
Sparse Core Ops, SparseCore 0:
  10.5 76.1 all-gather.1
  99.0 72.5 all-reduce.5
  242.3 84.0 all-reduce.7
  330.9 143.6 all-reduce.9
  478.6 82.4 reduce-scatter.4
  565.2 100.8 reduce-scatter.2
where the time goes:
time: 677 us; the launch traced here: 675 us
  waiting for transfers between devices  409 us (60%)
  blocking collectives  154 us (23%)
  matrix products  58.3 us (9%)
  other arithmetic  34.4 us (5%)
  between operations  14.2 us (2%)
    reduce_scatter x1, waiting for transfers between devices, on_device(): lax.psum_scatter(inner(tokens, dpre).astype(jnp.bfloat16), 'row', scatter...  103 us
    psum x1, waiting for transfers between devices, on_device(): dnorm = lax.psum(dnorm_part, 'proto')  84.1 us
    reduce_scatter x1, waiting for transfers between devices, on_device(): lax.psum_scatter(inner(student_n, grad_s).astype(jnp.bfloat16), 'row', sc...  84.1 us
    psum x1, blocking collectives, on_device(): loss = lax.psum(jnp.sum(weight * cross), ('row', 'proto'))  67.4 us
    psum x1, waiting for transfers between devices, on_device(): lax.psum(inner(hidden, dbott).astype(jnp.bfloat16), 'row')  57.7 us
    all_gather x1, waiting for transfers between devices, on_device(): lax.all_gather(w_in, 'row', axis=0, tiled=True)  40.6 us
    psum x1, waiting for transfers between devices, on_device(): bott = lax.psum(partial_value, 'proto')  38.4 us
    psum x1, blocking collectives, on_device(): counts = lax.psum(jnp.sum(onehot, axis=0), 'row')  34.7 us
  transfers between devices with their start and end apart: 6, of which 6 were waited for; matrix products, arithmetic and copies ran while one was open for 5% of the time, Pallas kernels for 0%

commit v1 on v0

v1 whole, which is shorter than its diff:
```python
import jax
import jax.numpy as jnp
from jax import lax
from jax.sharding import PartitionSpec as P
from jax.experimental import pallas as pl
from jax.experimental.pallas import tpu as pltpu

tau_teacher = 0.07
tau_student = 0.1
loss_scale = 1048576.0
norm_eps = 1e-06
MESH = pl.DeviceIdType.MESH
VMEM = pltpu.VMEM
f32 = jnp.float32
bf16 = jnp.bfloat16


def vspec():
    return pl.BlockSpec(memory_space=pltpu.VMEM)


def aspec():
    return pl.BlockSpec(memory_space=pl.ANY)


class Place:
    def __init__(self):
        self.r = lax.axis_index("row")
        self.p = lax.axis_index("proto")
        self.xh = self.r // 8
        self.y = (self.r // 2) % 4
        self.c = self.r % 2

    def chip(self, other, dy):
        fam = 1 - self.xh if other else self.xh
        return fam * 4 + (self.y + dy) % 4

    def slot(self, other, dy, core=None):
        return self.chip(other, dy) * 2 + (self.c if core is None else core)

    def dev(self, row):
        return (row, self.p)

    @property
    def X(self):
        return self.dev(self.slot(True, 0))

    @property
    def YP(self):
        return self.dev(self.slot(False, 1))

    @property
    def YM(self):
        return self.dev(self.slot(False, 3))

    @property
    def CO(self):
        return self.dev(self.slot(False, 0, 1 - self.c))

    def row_peer(self, d):
        return ((self.r + d) % 16, self.p)

    def proto_peer(self, d):
        return (self.r, (self.p + d) % 8)


class Copies:
    def __init__(self, send, recv):
        self.send, self.recv, self.all = send, recv, []

    def start(self, src, dst, dev):
        i = len(self.all)
        cp = pltpu.make_async_remote_copy(
            src_ref=src,
            dst_ref=dst,
            send_sem=self.send.at[i],
            recv_sem=self.recv.at[i],
            device_id=dev,
            device_id_type=MESH,
        )
        cp.start()
        self.all.append(cp)
        return cp

    def finish(self):
        for cp in self.all:
            cp.wait_send()


def greet(peers):
    bar = pltpu.get_barrier_semaphore()
    for dev in peers:
        pl.semaphore_signal(bar, inc=1, device_id=dev, device_id_type=MESH)


def met(count):
    pl.semaphore_wait(pltpu.get_barrier_semaphore(), count)


def gather_rows(cps, at, own, buf, a, h, al, work, tail=None):
    n = buf.shape[1]
    up, lo = pl.ds(h, n - h), pl.ds(0, h)
    A, B = pl.ds(0, a), pl.ds(a, n - a)
    aup, alo = pl.ds(al, a - al), pl.ds(0, al)
    me = at.slot(False, 0)
    x0 = cps.start(own, buf.at[me], at.X)
    p0 = cps.start(own, buf.at[me], at.YP)
    m0 = cps.start(own, buf.at[me], at.YM)
    c0 = cps.start(own, buf.at[me], at.CO)
    work("start", None)
    sx = at.slot(True, 0)
    sm, sp, sf = at.slot(False, 3), at.slot(False, 1), at.slot(False, 2)
    xm, xp, xf = at.slot(True, 3), at.slot(True, 1), at.slot(True, 2)
    x0.wait_recv()
    xap = cps.start(buf.at[sx, A], buf.at[sx, A], at.YP)
    xam = cps.start(buf.at[sx, A], buf.at[sx, A], at.YM)
    xc = cps.start(buf.at[sx], buf.at[sx], at.CO)
    p0.wait_recv()
    fup = cps.start(buf.at[sm, up], buf.at[sm, up], at.YP)
    bm = cps.start(buf.at[sm, B], buf.at[sm, B], at.X)
    cm = cps.start(buf.at[sm], buf.at[sm], at.CO)
    m0.wait_recv()
    flo = cps.start(buf.at[sp, lo], buf.at[sp, lo], at.YM)
    bp = cps.start(buf.at[sp, B], buf.at[sp, B], at.X)
    cp = cps.start(buf.at[sp], buf.at[sp], at.CO)
    c0.wait_recv()
    work("chip", at.chip(False, 0))
    xc.wait_recv()
    work("chip", at.chip(True, 0))
    fup.wait_recv()
    flo.wait_recv()
    bf = cps.start(buf.at[sf, B], buf.at[sf, B], at.X)
    cf = cps.start(buf.at[sf], buf.at[sf], at.CO)
    xap.wait_recv()
    gup = cps.start(buf.at[xm, aup], buf.at[xm, aup], at.YP)
    xam.wait_recv()
    glo = cps.start(buf.at[xp, alo], buf.at[xp, alo], at.YM)
    bm.wait_recv()
    cxm = cps.start(buf.at[xm], buf.at[xm], at.CO)
    bp.wait_recv()
    cxp = cps.start(buf.at[xp], buf.at[xp], at.CO)
    cm.wait_recv()
    work("chip", at.chip(False, 3))
    cp.wait_recv()
    work("chip", at.chip(False, 1))
    cf.wait_recv()
    work("chip", at.chip(False, 2))
    cxm.wait_recv()
    work("chip", at.chip(True, 3))
    cxp.wait_recv()
    work("chip", at.chip(True, 1))
    gup.wait_recv()
    glo.wait_recv()
    bf.wait_recv()
    cxf = cps.start(buf.at[xf], buf.at[xf], at.CO)
    cxf.wait_recv()
    work("chip", at.chip(True, 2))


def gelu_parts(values):
    cumul = 0.5 * (1.0 + lax.erf(values * 0.7071067811865476))
    density = jnp.exp(-0.5 * values * values) * 0.3989422804014327
    return (values * cumul, cumul + values * density)


def head_kernel(
    tokens, w_in, w_out, teacher, proto_t, center, img,
    hid_o, slope_o, sn_o, unit_o, recip_o, et_o, mt_o, st_o, wt_o,
    tok, wbuf, pt, lt, pre, tbuf, cbuf, part, rbuf, sbuf, send, recv, lsem,
):
    at = Place()
    cps = Copies(send, recv)
    rows, depth = tok.shape
    peers = [at.row_peer(d) for d in range(1, 16)] + [at.proto_peer(d) for d in range(1, 8)]
    greet(peers)
    me = at.slot(False, 0)
    own = pltpu.make_async_copy(w_in, wbuf.at[me], lsem.at[0])
    own.start()
    load_pt = pltpu.make_async_copy(proto_t, pt, lsem.at[1])
    load_pt.start()
    load_tok = pltpu.make_async_copy(tokens, tok, lsem.at[2])
    load_tok.start()
    lanes = lax.broadcasted_iota(jnp.int32, img.shape, 1)
    onehot = (img[...] == lanes).astype(f32)
    cbuf[at.r] = jnp.broadcast_to(jnp.sum(onehot, axis=0, keepdims=True), (8, 128))
    t = teacher[...].astype(f32)
    tbuf[at.p] = (t * lax.rsqrt(jnp.sum(t * t, axis=1, keepdims=True) + norm_eps)).astype(bf16)
    pre[...] = jnp.zeros_like(pre)
    met(len(peers))

    def scores():
        tc = [cps.start(tbuf.at[at.p], tbuf.at[at.p], at.proto_peer(d)) for d in range(1, 8)]
        cc = [cps.start(cbuf.at[at.r], cbuf.at[at.r], at.row_peer(d)) for d in range(1, 16)]
        load_pt.wait()
        for k in tc:
            k.wait_recv()
        tn = tbuf[...].reshape(rows, tbuf.shape[2])
        step = 512

        def one(j, top):
            cols = pl.ds(pl.multiple_of(j * step, step), step)
            v = jnp.dot(tn, pt[:, cols], preferred_element_type=f32)
            v = (v - center[:, cols]) * (1.0 / tau_teacher)
            lt[:, cols] = v
            for q in range(step // 128):
                top = jnp.maximum(top, v[:, q * 128 : (q + 1) * 128])
            return top

        mt_o[...] = lax.fori_loop(
            0, lt.shape[1] // step, one, jnp.full((rows, 128), -jnp.inf, f32)
        )
        mt_o[...] = jnp.broadcast_to(jnp.max(mt_o[...], axis=1, keepdims=True), (rows, 128))
        st_o[...] = jnp.zeros_like(st_o)

        def two(j, _):
            cols = pl.ds(pl.multiple_of(j * 128, 128), 128)
            e = jnp.exp(lt[:, cols] - mt_o[...])
            lt[:, cols] = e
            st_o[...] += e
            return 0

        lax.fori_loop(0, lt.shape[1] // 128, two, 0)
        for k in cc:
            k.wait_recv()
        counts = jnp.sum(cbuf[...], axis=0)[0:1]
        per_row = jnp.sum(onehot * counts, axis=1, keepdims=True)
        wt_o[...] = jnp.broadcast_to(1.0 / (64.0 * per_row), wt_o.shape)

    save = pltpu.make_async_copy(lt, et_o, lsem.at[3])

    def work(kind, chip):
        if kind == "start":
            scores()
            save.start()
            own.wait()
            load_tok.wait()
            return
        block = wbuf.shape[1] * 2
        lhs = tok[:, pl.ds(pl.multiple_of(chip * block, block), block)]

        def tile(j, _):
            cols = pl.ds(pl.multiple_of(j * 256, 256), 256)
            rhs = wbuf[pl.ds(chip * 2, 2), :, cols].reshape(block, 256)
            pre[:, cols] += jnp.dot(lhs, rhs, preferred_element_type=f32)
            return 0

        lax.fori_loop(0, pre.shape[1] // 256, tile, 0)

    gather_rows(cps, at, w_in, wbuf, 144, 128, 64, work)

    small = part.shape[1]

    def act(i, _):
        rs = pl.ds(pl.multiple_of(i * small, small), small)
        value, slope = gelu_parts(pre[rs, :])
        slope_o[rs, :] = slope
        h = value.astype(bf16)
        hid_o[rs, :] = h
        part[i] = jnp.dot(h, w_out[...], preferred_element_type=f32)
        return 0

    lax.fori_loop(0, rows // small, act, 0)
    rc = [
        cps.start(part.at[(at.p + d) % 8], rbuf.at[d], at.proto_peer(d)) for d in range(1, 8)
    ]
    total = part[at.p]
    for d in range(1, 8):
        rc[d - 1].wait_recv()
        total = total + rbuf[d]
    recip = lax.rsqrt(jnp.sum(total * total, axis=1, keepdims=True) + norm_eps)
    unit = total * recip
    unit_o[...] = unit
    recip_o[...] = jnp.broadcast_to(recip, recip_o.shape)
    sbuf[at.p] = unit.astype(bf16)
    sc = [cps.start(sbuf.at[at.p], sbuf.at[at.p], at.proto_peer(d)) for d in range(1, 8)]
    for k in sc:
        k.wait_recv()
    sn_o[...] = sbuf[...].reshape(rows, sbuf.shape[2])
    save.wait()
    cps.finish()


def head(tokens, w_in, w_out, teacher_z, proto_teacher, center, image_of):
    rows, depth = tokens.shape
    hid = w_in.shape[1]
    wide = w_out.shape[1]
    kk = proto_teacher.shape[1]
    img = jnp.broadcast_to(image_of[:, None], (rows, 128))
    small = teacher_z.shape[0]
    shp = jax.ShapeDtypeStruct
    copies = 20 + 7 + 15 + 7 + 7
    return pl.pallas_call(
        head_kernel,
        out_shape=(
            shp((rows, hid), bf16), shp((rows, hid), f32), shp((rows, wide), bf16),
            shp((small, wide), f32), shp((small, 128), f32), shp((rows, kk), f32),
            shp((rows, 128), f32), shp((rows, 128), f32), shp((rows, 128), f32),
        ),
        in_specs=[aspec(), aspec(), vspec(), vspec(), aspec(), vspec(), vspec()],
        out_specs=(vspec(),) * 5 + (aspec(),) + (vspec(),) * 3,
        scratch_shapes=[
            VMEM((rows, depth), bf16), VMEM((16,) + w_in.shape, bf16),
            VMEM(proto_teacher.shape, bf16), VMEM((rows, kk), f32), VMEM((rows, hid), f32),
            VMEM((8, small, wide), bf16), VMEM((16, 8, 128), f32), VMEM((8, small, wide), f32),
            VMEM((8, small, wide), f32), VMEM((8, small, wide), bf16),
            pltpu.SemaphoreType.DMA((copies,)), pltpu.SemaphoreType.DMA((copies,)),
            pltpu.SemaphoreType.DMA((4,)),
        ],
        compiler_params=pltpu.CompilerParams(
            collective_id=0, has_side_effects=True, vmem_limit_bytes=62 * 2**20
        ),
        name="head",
    )(tokens, w_in, w_out, teacher_z, proto_teacher, center[None, :], img)


def inner(left, right):
    return lax.dot_general(
        left, right, (((0,), (0,)), ((), ())), preferred_element_type=jnp.float32
    )


def outer_last(left, right):
    return lax.dot_general(
        left, right, (((1,), (1,)), ((), ())), preferred_element_type=jnp.float32
    )


def on_device(tokens, w_in, w_out, teacher_z, proto_student, proto_teacher, center, image_of):
    hidden, slope, student_n, unit, recip, exp_t, mt, st, wt = head(
        tokens, w_in, w_out, teacher_z, proto_teacher, center, image_of
    )
    recip = recip[:, :1]
    weight = wt[:, 0]
    local_t = mt[:, 0]
    logit_s = jnp.dot(student_n, proto_student, preferred_element_type=jnp.float32) / tau_student
    local_s = jnp.max(logit_s, axis=1)
    top_t, top_s = lax.pmax((local_t, local_s), "proto")
    fix = jnp.exp(local_t - top_t)
    exp_t = exp_t * fix[:, None]
    exp_s = jnp.exp(logit_s - top_s[:, None])
    total_t, total_s = lax.psum((jnp.sum(st, axis=1) * fix, jnp.sum(exp_s, axis=1)), "proto")
    prob_t = exp_t / total_t[:, None]
    prob_s = exp_s / total_s[:, None]
    logp_s = logit_s - top_s[:, None] - jnp.log(total_s)[:, None]
    cross = -jnp.sum(prob_t * logp_s, axis=1)
    loss = lax.psum(jnp.sum(weight * cross), ("row", "proto"))
    grad_s = (loss_scale * weight[:, None] * (prob_s - prob_t) / tau_student).astype(jnp.bfloat16)
    proto_grad = lax.psum_scatter(
        inner(student_n, grad_s).astype(jnp.bfloat16), "row", scatter_dimension=0, tiled=True
    ).astype(jnp.float32)
    dnorm = lax.psum_scatter(outer_last(grad_s, proto_student), "proto", scatter_dimension=0, tiled=True)
    dbott = (recip * (dnorm - unit * jnp.sum(unit * dnorm, axis=1, keepdims=True))).astype(bf16)
    dbott = lax.all_gather(dbott, "proto", axis=0, tiled=True)
    w_out_grad = lax.psum(inner(hidden, dbott).astype(jnp.bfloat16), "row").astype(jnp.float32)
    dpre = (outer_last(dbott, w_out) * slope).astype(jnp.bfloat16)
    w_in_grad = lax.psum_scatter(
        inner(tokens, dpre).astype(jnp.bfloat16), "row", scatter_dimension=0, tiled=True
    ).astype(jnp.float32)
    return (loss, w_in_grad, w_out_grad, proto_grad)


def solution(mesh):
    return jax.shard_map(
        on_device,
        mesh=mesh,
        in_specs=(
            P("row", None),
            P("row", "proto"),
            P("proto", None),
            P(("row", "proto"), None),
            P(None, "proto"),
            P(None, "proto"),
            P("proto"),
            P("row"),
        ),
        out_specs=(P(), P("row", "proto"), P("proto", None), P("row", "proto")),
        check_vma=False,
    )
```

time: 677 us -> 577 us (0.85)
  waiting for transfers between devices: 409 us -> 285 us
  Pallas kernels: 0 us -> 83 us
  blocking collectives: 154 us -> 124 us
  matrix products: 58.3 us -> 34 us
  other arithmetic: 34.4 us -> 27.5 us
    psum x2 -> x0, waiting for transfers between devices: 123 us -> none  [the longest x1 84.1 us: on_device(): dnorm = lax.psum(dnorm_part, 'proto')]
    pallas_call x0 -> x1, Pallas kernels: none -> 83 us  [head(): pl.pallas_call(head_kernel, out_shape=(shp((rows, hid), bf16), shp((rows,...]
    all_gather x1 -> x0, waiting for transfers between devices: 40.6 us -> none  [on_device(): lax.all_gather(w_in, 'row', axis=0, tiled=True)]
    reduce_scatter x0 -> x1, waiting for transfers between devices: none -> 39.8 us  [on_device(): lax.psum_scatter(outer_last(grad_s, proto_student), 'proto', scatter_dime...]
    psum x2 -> x1, blocking collectives: 47.4 us -> 12.7 us  [on_device(): lax.psum((jnp.sum(st, axis=1) * fix, jnp.sum(exp_s, axis=1)), 'proto')]
    dot_general x3 -> x0, matrix products: 21.2 us -> none  [the longest x1 10.6 us: on_device(): jnp.dot(tokens, lax.all_gather(w_in, 'row', axis=0, tiled=True), preferre...]
    psum x1, blocking collectives: 67.4 us -> 74.7 us  [on_device(): loss = lax.psum(jnp.sum(weight * cross), ('row', 'proto'))]
  transfers between devices with their start and end apart: 6 -> 4, of which waited for: 6 -> 4; matrix products, arithmetic and copies ran while one was open for 5% -> 4% of each run, Pallas kernels for 0% -> 0%
where the time goes in v1:
time: 577 us; the launch traced here: 575 us
  waiting for transfers between devices  285 us (49%)
  blocking collectives  124 us (21%)
  Pallas kernels  83 us (14%)
  matrix products  34 us (6%)
  other arithmetic  27.5 us (5%)
  between operations  13.9 us (2%)
  local copies, waits for them, and re-layouts  7.61 us (1%)
    reduce_scatter x1, waiting for transfers between devices, on_device(): lax.psum_scatter(inner(tokens, dpre).astype(jnp.bfloat16), 'row', scatter...  103 us
    reduce_scatter x1, waiting for transfers between devices, on_device(): lax.psum_scatter(inner(student_n, grad_s).astype(jnp.bfloat16), 'row', sc...  84.3 us
    pallas_call x1, Pallas kernels, head(): pl.pallas_call(head_kernel, out_shape=(shp((rows, hid), bf16), shp((rows,...  83 us
    psum x1, blocking collectives, on_device(): loss = lax.psum(jnp.sum(weight * cross), ('row', 'proto'))  74.7 us
    psum x1, waiting for transfers between devices, on_device(): lax.psum(inner(hidden, dbott).astype(jnp.bfloat16), 'row')  57.6 us
    reduce_scatter x1, waiting for transfers between devices, on_device(): lax.psum_scatter(outer_last(grad_s, proto_student), 'proto', scatter_dime...  39.8 us
    all_gather x1, blocking collectives, on_device(): dbott = lax.all_gather(dbott, 'proto', axis=0, tiled=True)  22.6 us
    dot_general x3, matrix products, inner(): lax.dot_general(left, right, (((0,), (0,)), ((), ())), preferred_element_...  19.3 us
  transfers between devices with their start and end apart: 4, of which 4 were waited for; matrix products, arithmetic and copies ran while one was open for 4% of the time, Pallas kernels for 0%

profile of v1, /device:TPU:1, one launch (start us, length us, event | category | flops | bytes accessed | tf_op | source)
XLA Modules:
  0.0 575.3 jit_solution(9380318522291462637)
XLA Ops:
  7.2 1.5 broadcast_in_dim.5.img
  8.7 83.0 %head.1 = (bf16[512,1024]{1,0:T(8,128)(2,1)}, f32[512,1024]{1,0:T(8,128)}, bf16[512,384]{1,0:T(8,128)(2,1)}, f32[64,384]{1,0:T(8,128)}, f32[64,128]{1,0:T(8,128)...) custom-call(bf16[512,4096]{1,0:T(8,128)(2,1)} %tokens.1, ...), custom_call_target="tpu_custom_call" | custom-call | tf_op jit(solution)/shard_map/head/pallas_call | solution.py:292
  91.8 1.2 multiply_reduce_fusion.2
  92.9 1.1 slice_reduce_fusion
  94.0 1.1 reduce_sum.45
  95.1 10.4 %multiply_reduce_fusion.1 = (f32[512]{0:T(512)S(1)}, f32[512,6144]{1,0:T(8,128)}) fusion(bf16[512,384]{1,0:T(8,128)(2,1)} %get-tuple-element.17, bf16[384,6144]{1,0:T(8,128)(2,1)} %param.12), kind=kOutput, calls=%fused_computation.5 | convolution fusion | flops 2422210048 | bytes 17696768 | tf_op jit(solution)/shard_map/dot_general | solution.py:335
  105.5 14.1 %all-reduce.1 = (f32[512]{0:T(512)S(1)}, f32[512]{0:T(512)S(1)}) all-reduce(f32[512]{0:T(512)S(1)} %get-tuple-element.40, f32[512]{0:T(512)S(1)} %slice_reduce_fusion), channel_id=1, replica_groups=mesh['row'=16,'proto'=8] {'proto'}, use_global_device_ids=true, to_apply=%region_4.0 | all-reduce | flops 1024 | bytes 8192 | tf_op jit(solution)/shard_map/pmax | solution.py:337
  119.6 6.8 %exponential_reduce_fusion = f32[512]{0:T(512)S(1)} fusion(f32[512,6144]{1,0:T(8,128)} %get-tuple-element.41, f32[512]{0:T(512)S(1)} %get-tuple-element.34), kind=kLoop, calls=%fused_computation.3 | loop fusion | flops 9436672 | bytes 12587008 | tf_op jit(solution)/shard_map/reduce_sum | solution.py:341
  126.4 12.7 %all-reduce = (f32[512]{0:T(512)S(1)}, f32[512]{0:T(512)S(1)}) all-reduce(f32[512]{0:T(512)S(1)} %exponential_reduce_fusion, f32[512]{0:T(512)S(1)} %get-tuple-element.36), channel_id=1, replica_groups=mesh['row'=16,'proto'=8] {'proto'}, use_global_device_ids=true, to_apply=%region_6.0 | all-reduce | flops 1024 | bytes 8192 | tf_op jit(solution)/shard_map/psum | solution.py:341
  139.2 11.6 %multiply_convert_fusion = (bf16[512,6144]{1,0:T(8,128)(2,1)S(1)}, f32[512]{0:T(512)S(1)}) fusion(f32[512,6144]{1,0:T(8,128)} %get-tuple-element.41, f32[512]{0:T(512)S(1)} %get-tuple-element.32, f32[512]{0:T(512)S(1)} %get-tuple-element.30, f32[512]{0:T(512)S(1)} %get-tuple-element.34, f32[512]{0:T(512)S(1)} %get-tuple-element.33, ...), kind=kLoop, calls=%fused_computation | loop fusion | flops 37748224 | bytes 31471616 | tf_op jit(solution)/shard_map/convert_element_type | solution.py:347
  150.9 2.6 copy-done
  153.5 4.3 fusion.1
  158.0 39.8 %reduce-scatter.4.cloned.1.call-done = f32[64,384]{1,0:T(8,128)} async-done(((f32[512,384]{1,0:T(8,128)}), f32[64,384]{1,0:T(8,128)}) %reduce-scatter.4.cloned.1.call-update) | async-done | bytes 98320 | tf_op jit(solution)/shard_map/reduce_scatter | solution.py:351
  199.8 22.6 %all_gather.3 = bf16[512,384]{1,0:T(8,128)(2,1)S(1)} all-gather(bf16[64,384]{1,0:T(8,128)(2,1)S(1)} %multiply_convert_fusion.2), channel_id=1, replica_groups=mesh['row'=16,'proto'=8] {'proto'}, dimensions={0}, use_global_device_ids=true | all-gather | bytes 442368 | tf_op jit(solution)/shard_map/all_gather | solution.py:353
  222.4 1.6 convolution_convert_fusion.1
  224.2 7.6 %convolution_convert_fusion = bf16[384,6144]{1,0:T(8,128)(2,1)} fusion(bf16[512,384]{1,0:T(8,128)(2,1)S(1)} %copy-done.1, bf16[512,6144]{1,0:T(8,128)(2,1)} %copy-done), kind=kOutput, calls=%fused_computation.6 | convolution fusion | flops 2418278400 | bytes 11403264 | tf_op jit(solution)/shard_map/dot_general | solution.py:317
  231.8 10.1 %convert_bitcast_fusion = bf16[4096,1024]{0,1:T(8,128)(2,1)} fusion(bf16[512,4096]{1,0:T(8,128)(2,1)} %tokens.1, f32[512,1024]{1,0:T(8,128)} %get-tuple-element.20, bf16[512,384]{1,0:T(8,128)(2,1)S(1)} %all_gather.3, bf16[1024,384]{1,0:T(8,128)(2,1)S(1)} %copy-done.2), kind=kOutput, calls=%fused_computation.7 | convolution fusion | flops 4702863360 | bytes 15859712 | tf_op jit(solution)/shard_map/dot_general | solution.py:317
  242.5 74.7 %psum.30 = f32[]{:T(128)} all-reduce(f32[]{:T(128)} %multiply_reduce_fusion.4), channel_id=1, replica_groups=mesh['row'=16,'proto'=8] {'row','proto'}, use_global_device_ids=true, to_apply=%region_9.0 | all-reduce | flops 1 | bytes 8 | tf_op jit(solution)/shard_map/psum | solution.py:346
  317.2 57.6 %all-reduce.4.cloned.1.call-done = bf16[1024,384]{1,0:T(8,128)(2,1)} async-done(((bf16[1024,384]{1,0:T(8,128)(2,1)}), bf16[1024,384]{1,0:T(8,128)(2,1)}) %all-reduce.4.cloned.1.call-update) | async-done | bytes 786448 | tf_op jit(solution)/shard_map/psum | solution.py:354
  374.8 2.4 convert_element_type.37
  377.2 84.3 %reduce-scatter.8.cloned.1.call-done = bf16[24,6144]{1,0:T(8,128)(2,1)} async-done(((bf16[384,6144]{1,0:T(8,128)(2,1)}), bf16[24,6144]{1,0:T(8,128)(2,1)}) %reduce-scatter.8.cloned.1.call-update) | async-done | bytes 294928 | tf_op jit(solution)/shard_map/reduce_scatter | solution.py:348
  461.5 1.8 convert_element_type.39
  463.3 103.2 %reduce-scatter.6.cloned.1.call-done = bf16[256,1024]{0,1:T(8,128)(2,1)} async-done(((bf16[4096,1024]{0,1:T(8,128)(2,1)}), bf16[256,1024]{0,1:T(8,128)(2,1)}) %reduce-scatter.6.cloned.1.call-update) | async-done | bytes 524304 | tf_op jit(solution)/shard_map/reduce_scatter | solution.py:356
  566.6 2.2 copy.13
  (30 shorter events, 3.0 us)
Async XLA Ops:
  7.2 190.6 %reduce-scatter.4.cloned.1.call-start = ((), (), s32[]{:S(2)}) async-start(), calls=%async_computation.3 | async-start | bytes 884736 | tf_op jit(solution)/shard_map/reduce_scatter | solution.py:351
  119.6 33.9 %slice-start = ((s8[4718592]{0:T(1024)(128)(4,1)}), s8[524288]{0:T(1024)(128)(4,1)S(1)}, s32[]{:S(2)}) async-start(s8[4718592]{0:T(1024)(128)(4,1)} %bitcast.14), calls=%async_computation.7 | async-start | bytes 1048576
  139.2 14.3 %slice-start.1 = ((s8[4718592]{0:T(1024)(128)(4,1)}), s8[4194304]{0:T(1024)(128)(4,1)S(1)}, s32[]{:S(2)}) async-start(s8[4718592]{0:T(1024)(128)(4,1)} %bitcast.14), calls=%async_computation.8 | async-start | bytes 8388608
  150.8 2.7 copy-start
  150.8 7.1 %copy-start.4 = (f32[64,128]{1,0:T(8,128)S(1)}, f32[64,128]{1,0:T(8,128)}, u32[]{:S(2)}) copy-start(f32[64,128]{1,0:T(8,128)} %get-tuple-element.18) | copy-start | bytes 98308
  150.8 46.9 %copy-start.3 = (f32[64,384]{1,0:T(8,128)S(1)}, f32[64,384]{1,0:T(8,128)}, u32[]{:S(2)}) copy-start(f32[64,384]{1,0:T(8,128)} %get-tuple-element.19) | copy-start | bytes 294916
  150.8 71.6 %copy-start.5 = (bf16[512,1024]{1,0:T(8,128)(2,1)S(1)}, bf16[512,1024]{1,0:T(8,128)(2,1)}, u32[]{:S(2)}) copy-start(bf16[512,1024]{1,0:T(8,128)(2,1)} %get-tuple-element.21) | copy-start | bytes 3145732
  150.9 73.3 %copy-start.1 = (bf16[512,384]{1,0:T(8,128)(2,1)S(1)}, bf16[512,384]{1,0:T(8,128)(2,1)}, u32[]{:S(2)}) copy-start(bf16[512,384]{1,0:T(8,128)(2,1)} %get-tuple-element.17) | copy-start | bytes 1179652
  157.8 74.0 %copy-start.2 = (bf16[1024,384]{1,0:T(8,128)(2,1)S(1)}, bf16[1024,384]{1,0:T(8,128)(2,1)}, u32[]{:S(2)}) copy-start(bf16[1024,384]{1,0:T(8,128)(2,1)} %w_out.1) | copy-start | bytes 2359300
  157.9 217.0 %all-reduce.4.cloned.1.call-start = ((), (), s32[]{:S(2)}) async-start(), calls=%async_computation.5 | async-start | bytes 1572864 | tf_op jit(solution)/shard_map/psum | solution.py:354
  224.1 237.4 %reduce-scatter.8.cloned.1.call-start = ((), (), s32[]{:S(2)}) async-start(), calls=%async_computation.6 | async-start | bytes 5013504 | tf_op jit(solution)/shard_map/reduce_scatter | solution.py:348
  231.8 334.8 %reduce-scatter.6.cloned.1.call-start = ((), (), s32[]{:S(2)}) async-start(), calls=%async_computation.4 | async-start | bytes 8912896 | tf_op jit(solution)/shard_map/reduce_scatter | solution.py:356
Sparse Core Ops, SparseCore 0:
  158.0 39.7 reduce-scatter.3
  224.2 150.5 all-reduce.3
  378.9 82.5 reduce-scatter.7
  465.6 100.8 reduce-scatter.5

commit v2 on v1

--- a/solution.py
+++ b/solution.py
@@ -97,70 +97,161 @@
     pl.semaphore_wait(pltpu.get_barrier_semaphore(), count)
 
 
-def gather_rows(cps, at, own, buf, a, h, al, work, tail=None):
+def gather_rows(cps, at, own, buf, a, h, al):
     n = buf.shape[1]
     up, lo = pl.ds(h, n - h), pl.ds(0, h)
     A, B = pl.ds(0, a), pl.ds(a, n - a)
     aup, alo = pl.ds(al, a - al), pl.ds(0, al)
+
+    def on(slot, part, dev):
+        ref = buf.at[slot] if part is None else buf.at[slot, part]
+        return cps.start(ref, ref, dev)
+
     me = at.slot(False, 0)
     x0 = cps.start(own, buf.at[me], at.X)
     p0 = cps.start(own, buf.at[me], at.YP)
     m0 = cps.start(own, buf.at[me], at.YM)
     c0 = cps.start(own, buf.at[me], at.CO)
-    work("start", None)
+    yield [(c0, at.chip(False, 0))]
     sx = at.slot(True, 0)
     sm, sp, sf = at.slot(False, 3), at.slot(False, 1), at.slot(False, 2)
     xm, xp, xf = at.slot(True, 3), at.slot(True, 1), at.slot(True, 2)
     x0.wait_recv()
-    xap = cps.start(buf.at[sx, A], buf.at[sx, A], at.YP)
-    xam = cps.start(buf.at[sx, A], buf.at[sx, A], at.YM)
-    xc = cps.start(buf.at[sx], buf.at[sx], at.CO)
+    xap = on(sx, A, at.YP)
+    xam = on(sx, A, at.YM)
+    xc = on(sx, None, at.CO)
     p0.wait_recv()
-    fup = cps.start(buf.at[sm, up], buf.at[sm, up], at.YP)
-    bm = cps.start(buf.at[sm, B], buf.at[sm, B], at.X)
-    cm = cps.start(buf.at[sm], buf.at[sm], at.CO)
+    fup = on(sm, up, at.YP)
+    bm = on(sm, B, at.X)
+    cm = on(sm, None, at.CO)
     m0.wait_recv()
-    flo = cps.start(buf.at[sp, lo], buf.at[sp, lo], at.YM)
-    bp = cps.start(buf.at[sp, B], buf.at[sp, B], at.X)
-    cp = cps.start(buf.at[sp], buf.at[sp], at.CO)
-    c0.wait_recv()
-    work("chip", at.chip(False, 0))
-    xc.wait_recv()
-    work("chip", at.chip(True, 0))
+    flo = on(sp, lo, at.YM)
+    bp = on(sp, B, at.X)
+    cp = on(sp, None, at.CO)
+    yield [(xc, at.chip(True, 0)), (cm, at.chip(False, 3)), (cp, at.chip(False, 1))]
     fup.wait_recv()
     flo.wait_recv()
-    bf = cps.start(buf.at[sf, B], buf.at[sf, B], at.X)
-    cf = cps.start(buf.at[sf], buf.at[sf], at.CO)
+    bf = on(sf, B, at.X)
+    cf = on(sf, None, at.CO)
     xap.wait_recv()
-    gup = cps.start(buf.at[xm, aup], buf.at[xm, aup], at.YP)
+    gup = on(xm, aup, at.YP)
     xam.wait_recv()
-    glo = cps.start(buf.at[xp, alo], buf.at[xp, alo], at.YM)
+    glo = on(xp, alo, at.YM)
     bm.wait_recv()
-    cxm = cps.start(buf.at[xm], buf.at[xm], at.CO)
+    cxm = on(xm, None, at.CO)
     bp.wait_recv()
-    cxp = cps.start(buf.at[xp], buf.at[xp], at.CO)
-    cm.wait_recv()
-    work("chip", at.chip(False, 3))
-    cp.wait_recv()
-    work("chip", at.chip(False, 1))
-    cf.wait_recv()
-    work("chip", at.chip(False, 2))
-    cxm.wait_recv()
-    work("chip", at.chip(True, 3))
-    cxp.wait_recv()
-    work("chip", at.chip(True, 1))
+    cxp = on(xp, None, at.CO)
+    yield [(cf, at.chip(False, 2)), (cxm, at.chip(True, 3)), (cxp, at.chip(True, 1))]
     gup.wait_recv()
     glo.wait_recv()
     bf.wait_recv()
-    cxf = cps.start(buf.at[xf], buf.at[xf], at.CO)
-    cxf.wait_recv()
-    work("chip", at.chip(True, 2))
+    cxf = on(xf, None, at.CO)
+    yield [(cxf, at.chip(True, 2))]
 
 
 def gelu_parts(values):
     cumul = 0.5 * (1.0 + lax.erf(values * 0.7071067811865476))
     density = jnp.exp(-0.5 * values * values) * 0.3989422804014327
     return (values * cumul, cumul + values * density)
+
+
+class Scatter:
+    def __init__(self, cps, at, S, bufs, axis, a, al, bl):
+        self.cps, self.at, self.S, self.axis = cps, at, S, axis
+        self.far, self.nm, self.np, self.xb, self.xa = bufs
+        n = S.shape[1 + axis]
+        self.A, self.B = (0, a), (a, n - a)
+        self.Alo, self.Aup = (0, al), (al, a - al)
+        self.Blo, self.Bup = (a, bl), (a + bl, n - a - bl)
+        self.got = {}
+
+    def idx(self, i, part):
+        cut = pl.ds(*part)
+        return (i, cut) if self.axis == 0 else (i, slice(None), cut)
+
+    def send(self, key, g, dst, i, part, dev):
+        self.got[key] = self.cps.start(
+            self.S.at[self.idx(g, part)], dst.at[self.idx(i, part)], dev
+        )
+
+    def add(self, g, part, *terms):
+        where = self.idx(g, part)
+        v = self.S[where].astype(f32)
+        for ref, i in terms:
+            v = v + ref[self.idx(i, part)].astype(f32)
+        self.S[where] = v.astype(bf16)
+
+    def wait(self, key):
+        self.got[key].wait_recv()
+
+    def ready(self, other, dy):
+        g, k = self.at.chip(other, dy), int(other)
+        if other:
+            self.send(("x", dy), g, self.xb, dy, self.B, self.at.X)
+        if dy == 2:
+            self.send(("fu", k), g, self.far, k, self.Aup, self.at.YP)
+            self.send(("fl", k), g, self.far, k, self.Alo, self.at.YM)
+        if dy == 1:
+            self.send(("ml", k), g, self.nm, k, self.Alo, self.at.YP)
+        if dy == 3:
+            self.send(("pu", k), g, self.np, k, self.Aup, self.at.YM)
+
+    def mid_a(self, k):
+        g1, g3 = self.at.chip(bool(k), 1), self.at.chip(bool(k), 3)
+        self.wait(("fu", k))
+        self.add(g1, self.Aup, (self.far, k))
+        self.send(("mu", k), g1, self.nm, k, self.Aup, self.at.YP)
+        self.wait(("fl", k))
+        self.add(g3, self.Alo, (self.far, k))
+        self.send(("pl", k), g3, self.np, k, self.Alo, self.at.YM)
+
+    def mid_b(self):
+        for dy in (2, 1, 3):
+            g = self.at.chip(False, dy)
+            self.wait(("x", dy))
+            self.add(g, self.B, (self.xb, dy))
+            if dy == 2:
+                self.send("bfu", g, self.far, 0, self.Bup, self.at.YP)
+                self.send("bfl", g, self.far, 0, self.Blo, self.at.YM)
+            elif dy == 1:
+                self.send("bml", g, self.nm, 0, self.Blo, self.at.YP)
+            else:
+                self.send("bpu", g, self.np, 0, self.Bup, self.at.YM)
+
+    def late_a(self):
+        for key in ("ml", "mu", "pl", "pu"):
+            self.wait((key, 1))
+        g = self.at.chip(True, 0)
+        self.add(g, self.A, (self.nm, 1), (self.np, 1))
+        self.send("xa", g, self.xa, 0, self.A, self.at.X)
+
+    def late_b(self):
+        g1, g3 = self.at.chip(False, 1), self.at.chip(False, 3)
+        self.wait("bfu")
+        self.add(g1, self.Bup, (self.far, 0))
+        self.send("bmu", g1, self.nm, 0, self.Bup, self.at.YP)
+        self.wait("bfl")
+        self.add(g3, self.Blo, (self.far, 0))
+        self.send("bpl", g3, self.np, 0, self.Blo, self.at.YM)
+
+    def final(self, fin):
+        g = self.at.chip(False, 0)
+        for key in ("ml", "mu", "pl", "pu"):
+            self.wait((key, 0))
+        for key in ("xa", ("x", 0), "bml", "bmu", "bpl", "bpu"):
+            self.wait(key)
+        for part, last, i in ((self.A, self.xa, 0), (self.B, self.xb, 0)):
+            v = self.S[self.idx(g, part)].astype(f32)
+            for ref, j in ((self.nm, 0), (self.np, 0), (last, i)):
+                v = v + ref[self.idx(j, part)].astype(f32)
+            fin[self.idx(0, part)[1:]] = v
+
+
+def scatter_bufs(shape):
+    return [VMEM((n,) + shape, bf16) for n in (2, 2, 2, 4, 1)]
+
+
+ORDER = [(True, 2), (True, 1), (True, 3), (True, 0), (False, 2), (False, 1), (False, 3), (False, 0)]
 
 
 def head_kernel(
@@ -228,13 +319,7 @@
 
     save = pltpu.make_async_copy(lt, et_o, lsem.at[3])
 
-    def work(kind, chip):
-        if kind == "start":
-            scores()
-            save.start()
-            own.wait()
-            load_tok.wait()
-            return
+    def accumulate(chip):
         block = wbuf.shape[1] * 2
         lhs = tok[:, pl.ds(pl.multiple_of(chip * block, block), block)]
 
@@ -246,7 +331,17 @@
 
         lax.fori_loop(0, pre.shape[1] // 256, tile, 0)
 
-    gather_rows(cps, at, w_in, wbuf, 144, 128, 64, work)
+    first = True
+    for landed in gather_rows(cps, at, w_in, wbuf, 144, 128, 64):
+        if first:
+            scores()
+            save.start()
+            own.wait()
+            load_tok.wait()
+            first = False
+        for copy, chip in landed:
+            copy.wait_recv()
+            accumulate(chip)
 
     small = part.shape[1]
 
@@ -313,50 +408,328 @@
     )(tokens, w_in, w_out, teacher_z, proto_teacher, center[None, :], img)
 
 
-def inner(left, right):
-    return lax.dot_general(
-        left, right, (((0,), (0,)), ((), ())), preferred_element_type=jnp.float32
+def across(row):
+    return jnp.transpose(jnp.broadcast_to(row, (128, row.shape[1])))
+
+
+def along(col):
+    return jnp.transpose(col)
+
+
+def middle_kernel(
+    sn, proto_s, et_in, mt, st, wt, unit, recip,
+    dbott_o, pgrad_o, loss_o,
+    ps, et, ls, gs, snt, ms, ss, cs, stats, fsb, ftb, S, snd, rc, far, nm, np_, xb, xa, fin, fcore,
+    dpart, drecv, dbuf, send, recv, lsem,
+):
+    at = Place()
+    cps = Copies(send, recv)
+    rows, kk = ls.shape
+    half = kk // 2
+    peers = [at.proto_peer(d) for d in range(1, 8)] + [at.X, at.YP, at.YM, at.CO]
+    greet(peers)
+    load_ps = pltpu.make_async_copy(proto_s, ps, lsem.at[0])
+    load_ps.start()
+    load_et = pltpu.make_async_copy(et_in, et, lsem.at[1])
+    load_et.start()
+    snt[...] = jnp.transpose(sn[...])
+    load_ps.wait()
+    step = 512
+
+    def one(j, top):
+        cols = pl.ds(pl.multiple_of(j * step, step), step)
+        v = jnp.dot(sn[...], ps[:, cols], preferred_element_type=f32) * (1.0 / tau_student)
+        ls[:, cols] = v
+        for q in range(step // 128):
+            top = jnp.maximum(top, v[:, q * 128 : (q + 1) * 128])
+        return top
+
+    ms[...] = lax.fori_loop(0, kk // step, one, jnp.full((rows, 128), -jnp.inf, f32))
+    ms[...] = jnp.broadcast_to(jnp.max(ms[...], axis=1, keepdims=True), (rows, 128))
+    ss[...] = jnp.zeros_like(ss)
+    cs[...] = jnp.zeros_like(cs)
+    load_et.wait()
+
+    def two(j, _):
+        cols = pl.ds(pl.multiple_of(j * 128, 128), 128)
+        d = ls[:, cols] - ms[...]
+        e = jnp.exp(d)
+        ls[:, cols] = e
+        ss[...] += e
+        cs[...] += et[:, cols] * d
+        return 0
+
+    lax.fori_loop(0, kk // 128, two, 0)
+    stats[at.p] = jnp.concatenate(
+        [
+            along(mt[...])[0:1],
+            jnp.sum(along(st[...]), axis=0, keepdims=True),
+            along(ms[...])[0:1],
+            jnp.sum(along(ss[...]), axis=0, keepdims=True),
+            jnp.sum(along(cs[...]), axis=0, keepdims=True),
+            jnp.zeros((3, rows), f32),
+        ],
+        axis=0,
     )
-
-
-def outer_last(left, right):
-    return lax.dot_general(
-        left, right, (((1,), (1,)), ((), ())), preferred_element_type=jnp.float32
+    met(len(peers))
+    sc = [cps.start(stats.at[at.p], stats.at[at.p], at.proto_peer(d)) for d in range(1, 8)]
+    for k in sc:
+        k.wait_recv()
+    table = [stats[q] for q in range(8)]
+    top_t = table[0][0:1]
+    top_s = table[0][2:3]
+    for q in table[1:]:
+        top_t = jnp.maximum(top_t, q[0:1])
+        top_s = jnp.maximum(top_s, q[2:3])
+    total_t = total_s = cross = jnp.zeros((1, rows), f32)
+    for q in table:
+        scale = jnp.exp(q[0:1] - top_t)
+        total_t = total_t + q[1:2] * scale
+        total_s = total_s + q[3:4] * jnp.exp(q[2:3] - top_s)
+        cross = cross + scale * (q[4:5] + q[1:2] * (q[2:3] - top_s))
+    cross = jnp.log(total_s) - cross / total_t
+    w_row = along(wt[...])[0:1]
+    loss_o[...] = jnp.broadcast_to(w_row * cross, loss_o.shape)
+    mine = stats[at.p]
+    lift = (loss_scale / tau_student) * w_row
+    fsb[...] = across(lift * jnp.exp(mine[2:3] - top_s) / total_s)
+    ftb[...] = across(lift * jnp.exp(mine[0:1] - top_t) / total_t)
+    dpart[...] = jnp.zeros_like(dpart)
+
+    def grads(base, dst):
+        def one(j, _):
+            first = base + j * step
+            for q in range(step // 128):
+                cols = pl.ds(pl.multiple_of(first + q * 128, 128), 128)
+                v = ls[:, cols] * fsb[...] - et[:, cols] * ftb[...]
+                gs[:, q * 128 : (q + 1) * 128] = v.astype(bf16)
+            cols = pl.ds(pl.multiple_of(first, step), step)
+            g = gs[...]
+            v = jnp.dot(snt[...], g, preferred_element_type=f32)
+            dst[:, :, pl.ds(pl.multiple_of(j * step, step), step)] = v.astype(bf16).reshape(
+                dst.shape[0], dst.shape[1], step
+            )
+            d = lax.dot_general(
+                g, ps[:, cols], (((1,), (1,)), ((), ())), preferred_element_type=f32
+            )
+            dpart[...] += d.reshape(dpart.shape)
+            return 0
+
+        lax.fori_loop(0, half // step, one, 0)
+
+    grads((1 - at.c) * half, snd)
+    swap = cps.start(snd, rc, at.CO)
+    grads(at.c * half, S)
+    dc = [
+        cps.start(dpart.at[(at.p + d) % 8], drecv.at[d], at.proto_peer(d)) for d in range(1, 8)
+    ]
+    swap.wait_recv()
+    rs = Scatter(cps, at, S, (far, nm, np_, xb, xa), 1, 1792, 768, 640)
+    for other, dy in ORDER:
+        g = at.chip(other, dy)
+        S[g] = (S[g].astype(f32) + rc[g].astype(f32)).astype(bf16)
+        rs.ready(other, dy)
+    rs.mid_a(1)
+    total = dpart[at.p]
+    for d in range(1, 8):
+        dc[d - 1].wait_recv()
+        total = total + drecv[d]
+    u, r = unit[...], recip[:, 0:1]
+    dbuf[at.p] = (r * (total - u * jnp.sum(u * total, axis=1, keepdims=True))).astype(bf16)
+    bc = [cps.start(dbuf.at[at.p], dbuf.at[at.p], at.proto_peer(d)) for d in range(1, 8)]
+    rs.mid_b()
+    rs.mid_a(0)
+    rs.late_a()
+    rs.late_b()
+    for k in bc:
+        k.wait_recv()
+    dbott_o[...] = dbuf[...].reshape(dbott_o.shape)
+    rs.final(fin)
+    n = fcore.shape[0]
+    keep, give = at.c * n, (1 - at.c) * n
+    fc = cps.start(fin.at[pl.ds(pl.multiple_of(give, 8), n)], fcore, at.CO)
+    pgrad_o[:, pl.ds(pl.multiple_of(at.c * half, half), half)] = fin[pl.ds(pl.multiple_of(keep, 8), n), :]
+    fc.wait_recv()
+    pgrad_o[:, pl.ds(pl.multiple_of((1 - at.c) * half, half), half)] = fcore[...]
+    cps.finish()
+
+
+def middle(sn, proto_s, et, mt, st, wt, unit, recip):
+    rows, wide = sn.shape
+    kk = proto_s.shape[1]
+    small = unit.shape[0]
+    shp = jax.ShapeDtypeStruct
+    chunk = (wide // 8, kk // 2)
+    copies = 7 + 1 + 7 + 7 + 23 + 1
+    lane = VMEM((rows, 128), f32)
+    return pl.pallas_call(
+        middle_kernel,
+        out_shape=(shp((rows, wide), bf16), shp((wide // 16, kk), f32), shp((8, rows), f32)),
+        in_specs=[vspec(), aspec(), aspec()] + [vspec()] * 5,
+        out_specs=(vspec(),) * 3,
+        scratch_shapes=[
+            VMEM((wide, kk), bf16), VMEM((rows, kk), f32), VMEM((rows, kk), f32), VMEM((rows, 512), bf16),
+            VMEM((wide, rows), bf16), lane, lane, lane, VMEM((8, 8, rows), f32), lane, lane,
+            VMEM((8,) + chunk, bf16), VMEM((8,) + chunk, bf16), VMEM((8,) + chunk, bf16),
+            *scatter_bufs(chunk), VMEM(chunk, f32), VMEM((chunk[0] // 2, chunk[1]), f32),
+            VMEM((8, small, wide), f32), VMEM((8, small, wide), f32), VMEM((8, small, wide), bf16),
+            pltpu.SemaphoreType.DMA((copies,)), pltpu.SemaphoreType.DMA((copies,)),
+            pltpu.SemaphoreType.DMA((2,)),
+        ],
+        compiler_params=pltpu.CompilerParams(
+            collective_id=1, has_side_effects=True, vmem_limit_bytes=62 * 2**20
+        ),
+        name="middle",
+    )(sn, proto_s, et, mt, st, wt, unit, recip)
+
+
+def tail_kernel(
+    tokens, hid, slope_in, dbott, w_out, loss_in,
+    wgrad_o, wout_o, loss_o,
+    tok, slope, dp, S, snd, rc, far, nm, np_, xb, xa, fin, fcore,
+    W, S2, rc2, far2, nm2, np2, xb2, xa2, fin2, own2, wbuf, lbuf, send, recv, lsem,
+):
+    at = Place()
+    cps = Copies(send, recv)
+    rows, hidden = dp.shape
+    half = hidden // 2
+    peers = [at.row_peer(d) for d in range(1, 16)]
+    greet(peers)
+    load_tok = pltpu.make_async_copy(tokens, tok, lsem.at[0])
+    load_tok.start()
+    load_slope = pltpu.make_async_copy(slope_in, slope, lsem.at[1])
+    load_slope.start()
+    lbuf[at.r] = jnp.broadcast_to(
+        jnp.sum(loss_in[...], axis=1, keepdims=True), lbuf.shape[1:]
     )
+    small = W.shape[2]
+    for j in range(hidden // 256):
+        cols = slice(j * 256, (j + 1) * 256)
+        v = lax.dot_general(
+            hid[:, cols], dbott[...], (((0,), (0,)), ((), ())), preferred_element_type=f32
+        ).astype(bf16)
+        for i in range(256 // small):
+            k = j * (256 // small) + i
+            W[k % 2, k // 2] = v[i * small : (i + 1) * small]
+    met(len(peers))
+    lc = [cps.start(lbuf.at[at.r], lbuf.at[at.r], at.row_peer(d)) for d in range(1, 16)]
+    swap2 = cps.start(W.at[1 - at.c], rc2, at.CO)
+    load_slope.wait()
+
+    def back(j, _):
+        cols = pl.ds(pl.multiple_of(j * 256, 256), 256)
+        v = lax.dot_general(
+            dbott[...], w_out[cols, :], (((1,), (1,)), ((), ())), preferred_element_type=f32
+        )
+        dp[:, cols] = (v * slope[:, cols]).astype(bf16)
+        return 0
+
+    lax.fori_loop(0, hidden // 256, back, 0)
+    load_tok.wait()
+    rs = Scatter(cps, at, S, (far, nm, np_, xb, xa), 0, 288, 128, 112)
+    rs2 = Scatter(cps, at, S2, (far2, nm2, np2, xb2, xa2), 0, 32, 16, 16)
+    swaps = {}
+
+    def chunk(other, dy):
+        g = at.chip(other, dy)
+        lhs = pl.ds(pl.multiple_of(g * 512, 512), 512)
+        for dst, side in ((snd, 1 - at.c), (S, at.c)):
+            rhs = pl.ds(pl.multiple_of(side * half, half), half)
+            dst[g] = lax.dot_general(
+                tok[:, lhs], dp[:, rhs], (((0,), (0,)), ((), ())), preferred_element_type=f32
+            ).astype(bf16)
+            if dst is snd:
+                swaps[other, dy] = cps.start(snd.at[g], rc.at[g], at.CO)
+
+    def merge(other, dy):
+        g = at.chip(other, dy)
+        swaps[other, dy].wait_recv()
+        S[g] = (S[g].astype(f32) + rc[g].astype(f32)).astype(bf16)
+        rs.ready(other, dy)
+
+    for i, key in enumerate(ORDER):
+        chunk(*key)
+        if i > 0:
+            merge(*ORDER[i - 1])
+        if i == 1:
+            swap2.wait_recv()
+            S2[...] = (W[at.c].astype(f32) + rc2[...].astype(f32)).astype(bf16)
+            for k2 in ORDER:
+                rs2.ready(*k2)
+        if i == 3:
+            rs2.mid_a(1)
+            rs2.mid_b()
+            rs2.mid_a(0)
+        if i == 5:
+            rs.mid_a(1)
+            rs2.late_a()
+            rs2.late_b()
+    merge(*ORDER[-1])
+    rs2.final(fin2)
+    own2[...] = fin2[...].astype(bf16)
+    wbuf[at.r] = own2[...]
+    gather = gather_rows(cps, at, own2, wbuf, 32, 32, 16)
+    landed = list(next(gather))
+    rs.mid_b()
+    rs.mid_a(0)
+    landed += next(gather)
+    rs.late_a()
+    landed += next(gather)
+    rs.late_b()
+    landed += next(gather)
+    rs.final(fin)
+    n = fcore.shape[0]
+    fc = cps.start(fin.at[pl.ds(pl.multiple_of((1 - at.c) * n, n), n)], fcore, at.CO)
+    wgrad_o[:, pl.ds(pl.multiple_of(at.c * half, half), half)] = fin[pl.ds(pl.multiple_of(at.c * n, n), n), :]
+    for copy, _ in landed:
+        copy.wait_recv()
+    wout_o[...] = wbuf[...].astype(f32).reshape(wout_o.shape)
+    for k in lc:
+        k.wait_recv()
+    loss_o[...] = jnp.sum(lbuf[...], axis=0)
+    fc.wait_recv()
+    wgrad_o[:, pl.ds(pl.multiple_of((1 - at.c) * half, half), half)] = fcore[...]
+    cps.finish()
+
+
+def tail(tokens, hid, slope, dbott, w_out, loss_row):
+    rows, depth = tokens.shape
+    hidden, wide = w_out.shape
+    shp = jax.ShapeDtypeStruct
+    block = (depth // 8, hidden // 2)
+    small = (hidden // 16, wide)
+    copies = 15 + 1 + 8 + 23 + 23 + 20 + 1
+    return pl.pallas_call(
+        tail_kernel,
+        out_shape=(shp((depth // 16, hidden), f32), shp((hidden, wide), f32), shp((8, 128), f32)),
+        in_specs=[aspec(), vspec(), aspec(), vspec(), vspec(), vspec()],
+        out_specs=(vspec(),) * 3,
+        scratch_shapes=[
+            VMEM((rows, depth), bf16), VMEM((rows, hidden), f32), VMEM((rows, hidden), bf16),
+            VMEM((8,) + block, bf16), VMEM((8,) + block, bf16), VMEM((8,) + block, bf16),
+            *scatter_bufs(block), VMEM(block, f32), VMEM((block[0] // 2, block[1]), f32),
+            VMEM((2, 8) + small, bf16), VMEM((8,) + small, bf16), VMEM((8,) + small, bf16),
+            *scatter_bufs(small), VMEM(small, f32), VMEM(small, bf16), VMEM((16,) + small, bf16),
+            VMEM((16, 8, 128), f32),
+            pltpu.SemaphoreType.DMA((copies,)), pltpu.SemaphoreType.DMA((copies,)),
+            pltpu.SemaphoreType.DMA((2,)),
+        ],
+        compiler_params=pltpu.CompilerParams(
+            collective_id=2, has_side_effects=True, vmem_limit_bytes=62 * 2**20
+        ),
+        name="tail",
+    )(tokens, hid, slope, dbott, w_out, loss_row)
 
 
 def on_device(tokens, w_in, w_out, teacher_z, proto_student, proto_teacher, center, image_of):
     hidden, slope, student_n, unit, recip, exp_t, mt, st, wt = head(
         tokens, w_in, w_out, teacher_z, proto_teacher, center, image_of
     )
-    recip = recip[:, :1]
-    weight = wt[:, 0]
-    local_t = mt[:, 0]
-    logit_s = jnp.dot(student_n, proto_student, preferred_element_type=jnp.float32) / tau_student
-    local_s = jnp.max(logit_s, axis=1)
-    top_t, top_s = lax.pmax((local_t, local_s), "proto")
-    fix = jnp.exp(local_t - top_t)
-    exp_t = exp_t * fix[:, None]
-    exp_s = jnp.exp(logit_s - top_s[:, None])
-    total_t, total_s = lax.psum((jnp.sum(st, axis=1) * fix, jnp.sum(exp_s, axis=1)), "proto")
-    prob_t = exp_t / total_t[:, None]
-    prob_s = exp_s / total_s[:, None]
-    logp_s = logit_s - top_s[:, None] - jnp.log(total_s)[:, None]
-    cross = -jnp.sum(prob_t * logp_s, axis=1)
-    loss = lax.psum(jnp.sum(weight * cross), ("row", "proto"))
-    grad_s = (loss_scale * weight[:, None] * (prob_s - prob_t) / tau_student).astype(jnp.bfloat16)
-    proto_grad = lax.psum_scatter(
-        inner(student_n, grad_s).astype(jnp.bfloat16), "row", scatter_dimension=0, tiled=True
-    ).astype(jnp.float32)
-    dnorm = lax.psum_scatter(outer_last(grad_s, proto_student), "proto", scatter_dimension=0, tiled=True)
-    dbott = (recip * (dnorm - unit * jnp.sum(unit * dnorm, axis=1, keepdims=True))).astype(bf16)
-    dbott = lax.all_gather(dbott, "proto", axis=0, tiled=True)
-    w_out_grad = lax.psum(inner(hidden, dbott).astype(jnp.bfloat16), "row").astype(jnp.float32)
-    dpre = (outer_last(dbott, w_out) * slope).astype(jnp.bfloat16)
-    w_in_grad = lax.psum_scatter(
-        inner(tokens, dpre).astype(jnp.bfloat16), "row", scatter_dimension=0, tiled=True
-    ).astype(jnp.float32)
-    return (loss, w_in_grad, w_out_grad, proto_grad)
+    dbott, proto_grad, loss_row = middle(
+        student_n, proto_student, exp_t, mt, st, wt, unit, recip
+    )
+    w_in_grad, w_out_grad, loss = tail(tokens, hidden, slope, dbott, w_out, loss_row)
+    return (loss[0, 0], w_in_grad, w_out_grad, proto_grad)
 
 
 def solution(mesh):

time: 577 us -> 214 us (0.37)
  waiting for transfers between devices: 285 us -> 0 us
  blocking collectives: 124 us -> 0 us
  Pallas kernels: 83 us -> 204 us
  matrix products: 34 us -> 0 us
  other arithmetic: 27.5 us -> 0 us
  between operations: 13.9 us -> 0.67 us
    reduce_scatter x3 -> x0, waiting for transfers between devices: 227 us -> none  [the longest x1 103 us: on_device(): lax.psum_scatter(inner(tokens, dpre).astype(jnp.bfloat16), 'row', scatter...]
    pallas_call x0 -> x2, Pallas kernels: none -> 120 us  [the longest x1 64.7 us: middle(): pl.pallas_call(middle_kernel, out_shape=(shp((rows, wide), bf16), shp((wi...]
    psum x2 -> x0, blocking collectives: 87.4 us -> none  [the longest x1 74.7 us: on_device(): loss = lax.psum(jnp.sum(weight * cross), ('row', 'proto'))]
    psum x1 -> x0, waiting for transfers between devices: 57.6 us -> none  [on_device(): lax.psum(inner(hidden, dbott).astype(jnp.bfloat16), 'row')]
    dot_general x5 -> x0, matrix products: 34 us -> none  [the longest x3 19.3 us: inner(): lax.dot_general(left, right, (((0,), (0,)), ((), ())), preferred_element_...]
    all_gather x1 -> x0, blocking collectives: 22.6 us -> none  [on_device(): dbott = lax.all_gather(dbott, 'proto', axis=0, tiled=True)]
    convert_element_type x4 -> x0, other arithmetic: 16.8 us -> none  [the longest x1 11.6 us: on_device(): (loss_scale * weight[:, None] * (prob_s - prob_t) / tau_student).astype(j...]
    pmax x1 -> x0, blocking collectives: 14.1 us -> none  [on_device(): top_t, top_s = lax.pmax((local_t, local_s), 'proto')]
  transfers between devices with their start and end apart: 4 -> 0, of which waited for: 4 -> 0; matrix products, arithmetic and copies ran while one was open for 4% -> 0% of each run, Pallas kernels for 0% -> 0%
where the time goes in v2:
time: 214 us; the launch traced here: 213 us
  Pallas kernels  204 us (95%)
  local copies, waits for them, and re-layouts  8.54 us (4%)
    pallas_call x1, Pallas kernels, head(): pl.pallas_call(head_kernel, out_shape=(shp((rows, hid), bf16), shp((rows,...  83.7 us
    pallas_call x1, Pallas kernels, middle(): pl.pallas_call(middle_kernel, out_shape=(shp((rows, wide), bf16), shp((wi...  64.7 us
    pallas_call x1, Pallas kernels, tail(): pl.pallas_call(tail_kernel, out_shape=(shp((depth // 16, hidden), f32), s...  55.7 us
    unnamed x5, local copies, waits for them, and re-layouts  5.78 us

profile of v2, /device:TPU:1, one launch (start us, length us, event | category | flops | bytes accessed | tf_op | source)
XLA Modules:
  0.0 213.3 jit_solution(17554217368919495539)
XLA Ops:
  0.6 1.5 broadcast_in_dim.10.img
  2.1 83.7 %head.1 = (bf16[512,1024]{1,0:T(8,128)(2,1)}, f32[512,1024]{1,0:T(8,128)}, bf16[512,384]{1,0:T(8,128)(2,1)}, f32[64,384]{1,0:T(8,128)}, f32[64,128]{1,0:T(8,128)...) custom-call(bf16[512,4096]{1,0:T(8,128)(2,1)} %tokens.3, ...), custom_call_target="tpu_custom_call" | custom-call | tf_op jit(solution)/shard_map/head/pallas_call | solution.py:387
  85.9 64.7 %middle.1 = (bf16[512,384]{1,0:T(8,128)(2,1)}, f32[24,6144]{1,0:T(8,128)}, f32[8,512]{1,0:T(8,128)}) custom-call(bf16[512,384]{1,0:T(8,128)(2,1)} %get-tuple-element.21.sn, bf16[384,6144]{1,0:T(8,128)(2,1)} %proto_s.1, f32[512,6144]{1,0:T(8,128)} %get-tuple-element.22.et_in, f32[512,128]{1,0:T(8,128)} %get-tuple-element.23.mt, ...), custom_call_target="tpu_custom_call" | custom-call | tf_op jit(solution)/shard_map/middle/pallas_call | solution.py:565
  150.6 55.7 %tail.1 = (f32[256,1024]{1,0:T(8,128)}, f32[1024,384]{1,0:T(8,128)}, f32[8,128]{1,0:T(8,128)}) custom-call(bf16[512,4096]{1,0:T(8,128)(2,1)} %tokens.3, bf16[512,1024]{1,0:T(8,128)(2,1)} %get-tuple-element.19.hid, f32[512,1024]{1,0:T(8,128)} %get-tuple-element.20.slope_in, bf16[512,384]{1,0:T(8,128)(2,1)} %get-tuple-element.28.dbott, ...), custom_call_target="tpu_custom_call" | custom-call | tf_op jit(solution)/shard_map/tail/pallas_call | solution.py:702
  206.3 0.0 copy-start
  206.3 1.2 slice.3
  207.5 2.3 %copy.15 = f32[256,1024]{1,0:T(8,128)} copy(f32[256,1024]{1,0:T(8,128)} %get-tuple-element.39) | data formatting | bytes 2097152
  209.9 2.7 %copy.16 = f32[1024,384]{1,0:T(8,128)} copy(f32[1024,384]{1,0:T(8,128)} %get-tuple-element.40) | data formatting | bytes 3145728
  212.5 0.0 copy-done
  212.5 0.8 copy.17
Async XLA Ops:
  206.3 6.2 %copy-start = (f32[24,6144]{1,0:T(8,128)S(1)}, f32[24,6144]{1,0:T(8,128)}, u32[]{:S(2)}) copy-start(f32[24,6144]{1,0:T(8,128)} %get-tuple-element.41) | copy-start | bytes 1769476

commit v3 on v2

v3 whole, which is shorter than its diff:
```python
import jax
import jax.numpy as jnp
from jax import lax
from jax.sharding import PartitionSpec as P
from jax.experimental import pallas as pl
from jax.experimental.pallas import tpu as pltpu

tau_teacher = 0.07
tau_student = 0.1
loss_scale = 1048576.0
norm_eps = 1e-06
MESH = pl.DeviceIdType.MESH
VMEM = pltpu.VMEM
f32 = jnp.float32
bf16 = jnp.bfloat16


def vspec():
    return pl.BlockSpec(memory_space=pltpu.VMEM)


def aspec():
    return pl.BlockSpec(memory_space=pl.ANY)


class Place:
    def __init__(self):
        self.r = lax.axis_index("row")
        self.p = lax.axis_index("proto")
        self.xh = self.r // 8
        self.y = (self.r // 2) % 4
        self.c = self.r % 2

    def chip(self, other, dy):
        fam = 1 - self.xh if other else self.xh
        return fam * 4 + (self.y + dy) % 4

    def slot(self, other, dy, core=None):
        return self.chip(other, dy) * 2 + (self.c if core is None else core)

    def dev(self, row):
        return (row, self.p)

    @property
    def X(self):
        return self.dev(self.slot(True, 0))

    @property
    def YP(self):
        return self.dev(self.slot(False, 1))

    @property
    def YM(self):
        return self.dev(self.slot(False, 3))

    @property
    def CO(self):
        return self.dev(self.slot(False, 0, 1 - self.c))

    def row_peer(self, d):
        return ((self.r + d) % 16, self.p)

    def proto_peer(self, d):
        return (self.r, (self.p + d) % 8)


class Copies:
    def __init__(self, send, recv):
        self.send, self.recv, self.all = send, recv, []

    def start(self, src, dst, dev):
        i = len(self.all)
        cp = pltpu.make_async_remote_copy(
            src_ref=src,
            dst_ref=dst,
            send_sem=self.send.at[i],
            recv_sem=self.recv.at[i],
            device_id=dev,
            device_id_type=MESH,
        )
        cp.start()
        self.all.append(cp)
        return cp

    def expect(self, dst, i, dev):
        cp = pltpu.make_async_remote_copy(
            src_ref=dst,
            dst_ref=dst,
            send_sem=self.send.at[i],
            recv_sem=self.recv.at[i],
            device_id=dev,
            device_id_type=MESH,
        )
        self.all.append(cp)
        return cp

    def finish(self):
        for cp in self.all:
            cp.wait_send()


def greet(peers):
    bar = pltpu.get_barrier_semaphore()
    for dev in peers:
        pl.semaphore_signal(bar, inc=1, device_id=dev, device_id_type=MESH)


def met(count):
    pl.semaphore_wait(pltpu.get_barrier_semaphore(), count)


def gather_rows(cps, at, own, buf, base, n, a, h, al):
    every = (0, n)
    up, lo = (h, n - h), (0, h)
    A, B = (0, a), (a, n - a)
    aup, alo = (al, a - al), (0, al)

    def on(slot, part, dev, src=None):
        ref = buf.at[slot, pl.ds(base + part[0], part[1])]
        return cps.start(ref if src is None else src, ref, dev)

    me = at.slot(False, 0)
    mine = own.at[pl.ds(base, n)]
    x0 = on(me, every, at.X, mine)
    p0 = on(me, every, at.YP, mine)
    m0 = on(me, every, at.YM, mine)
    c0 = on(me, every, at.CO, mine)
    yield [(c0, at.chip(False, 0))]
    sx = at.slot(True, 0)
    sm, sp, sf = at.slot(False, 3), at.slot(False, 1), at.slot(False, 2)
    xm, xp, xf = at.slot(True, 3), at.slot(True, 1), at.slot(True, 2)
    x0.wait_recv()
    xap = on(sx, A, at.YP)
    xam = on(sx, A, at.YM)
    xc = on(sx, every, at.CO)
    p0.wait_recv()
    fup = on(sm, up, at.YP)
    bm = on(sm, B, at.X)
    cm = on(sm, every, at.CO)
    m0.wait_recv()
    flo = on(sp, lo, at.YM)
    bp = on(sp, B, at.X)
    cp = on(sp, every, at.CO)
    yield [(xc, at.chip(True, 0)), (cm, at.chip(False, 3)), (cp, at.chip(False, 1))]
    xap.wait_recv()
    gup = on(xm, aup, at.YP)
    xam.wait_recv()
    glo = on(xp, alo, at.YM)
    fup.wait_recv()
    flo.wait_recv()
    bf = on(sf, B, at.X)
    cf = on(sf, every, at.CO)
    bm.wait_recv()
    cxm = on(xm, every, at.CO)
    bp.wait_recv()
    cxp = on(xp, every, at.CO)
    yield [(cf, at.chip(False, 2)), (cxm, at.chip(True, 3)), (cxp, at.chip(True, 1))]
    gup.wait_recv()
    glo.wait_recv()
    bf.wait_recv()
    cxf = on(xf, every, at.CO)
    yield [(cxf, at.chip(True, 2))]


def across(row):
    return jnp.transpose(jnp.broadcast_to(row, (128, row.shape[1])))


def gelu_parts(values):
    cumul = 0.5 * (1.0 + lax.erf(values * 0.7071067811865476))
    density = jnp.exp(-0.5 * values * values) * 0.3989422804014327
    return (values * cumul, cumul + values * density)


class Scatter:
    def __init__(self, cps, at, S, bufs, axis, a, al, bl):
        self.cps, self.at, self.S, self.axis = cps, at, S, axis
        self.far, self.nm, self.np, self.xb, self.xa = bufs
        n = S.shape[1 + axis]
        self.A, self.B = (0, a), (a, n - a)
        self.Alo, self.Aup = (0, al), (al, a - al)
        self.Blo, self.Bup = (a, bl), (a + bl, n - a - bl)
        self.got = {}

    def idx(self, i, part):
        cut = pl.ds(*part)
        return (i, cut) if self.axis == 0 else (i, slice(None), cut)

    def send(self, key, g, dst, i, part, dev):
        self.got[key] = self.cps.start(
            self.S.at[self.idx(g, part)], dst.at[self.idx(i, part)], dev
        )

    def add(self, g, part, *terms):
        where = self.idx(g, part)
        v = self.S[where].astype(f32)
        for ref, i in terms:
            v = v + ref[self.idx(i, part)].astype(f32)
        self.S[where] = v.astype(bf16)

    def wait(self, key):
        self.got[key].wait_recv()

    def ready(self, other, dy):
        g, k = self.at.chip(other, dy), int(other)
        if dy == 2:
            self.send(("fu", k), g, self.far, k, self.Aup, self.at.YP)
            self.send(("fl", k), g, self.far, k, self.Alo, self.at.YM)
        if dy == 1:
            self.send(("ml", k), g, self.nm, k, self.Alo, self.at.YP)
        if dy == 3:
            self.send(("pu", k), g, self.np, k, self.Aup, self.at.YM)

    def ready_x(self, dy):
        self.send(("x", dy), self.at.chip(True, dy), self.xb, dy, self.B, self.at.X)

    def mid_a(self, k):
        g1, g3 = self.at.chip(bool(k), 1), self.at.chip(bool(k), 3)
        self.wait(("fu", k))
        self.add(g1, self.Aup, (self.far, k))
        self.send(("mu", k), g1, self.nm, k, self.Aup, self.at.YP)
        self.wait(("fl", k))
        self.add(g3, self.Alo, (self.far, k))
        self.send(("pl", k), g3, self.np, k, self.Alo, self.at.YM)

    def mid_b(self):
        for dy in (2, 1, 3):
            g = self.at.chip(False, dy)
            self.wait(("x", dy))
            self.add(g, self.B, (self.xb, dy))
            if dy == 2:
                self.send("bfu", g, self.far, 0, self.Bup, self.at.YP)
                self.send("bfl", g, self.far, 0, self.Blo, self.at.YM)
            elif dy == 1:
                self.send("bml", g, self.nm, 0, self.Blo, self.at.YP)
            else:
                self.send("bpu", g, self.np, 0, self.Bup, self.at.YM)

    def late_a(self):
        for key in ("ml", "mu", "pl", "pu"):
            self.wait((key, 1))
        g = self.at.chip(True, 0)
        self.add(g, self.A, (self.nm, 1), (self.np, 1))
        self.send("xa", g, self.xa, 0, self.A, self.at.X)

    def late_b(self):
        g1, g3 = self.at.chip(False, 1), self.at.chip(False, 3)
        self.wait("bfu")
        self.add(g1, self.Bup, (self.far, 0))
        self.send("bmu", g1, self.nm, 0, self.Bup, self.at.YP)
        self.wait("bfl")
        self.add(g3, self.Blo, (self.far, 0))
        self.send("bpl", g3, self.np, 0, self.Blo, self.at.YM)

    def final(self, fin):
        g = self.at.chip(False, 0)
        for key in ("ml", "mu", "pl", "pu"):
            self.wait((key, 0))
        for key in ("xa", ("x", 0), "bml", "bmu", "bpl", "bpu"):
            self.wait(key)
        for part, last, i in ((self.A, self.xa, 0), (self.B, self.xb, 0)):
            v = self.S[self.idx(g, part)].astype(f32)
            for ref, j in ((self.nm, 0), (self.np, 0), (last, i)):
                v = v + ref[self.idx(j, part)].astype(f32)
            fin[self.idx(0, part)[1:]] = v


def scatter_bufs(shape):
    return [VMEM((n,) + shape, bf16) for n in (2, 2, 2, 4, 1)]


ORDER = [(True, 2), (True, 1), (True, 3), (True, 0), (False, 2), (False, 1), (False, 3), (False, 0)]


def head_kernel(
    tokens, w_in, w_out, teacher, proto_t, center,
    hid_o, slope_o, sn_o, unit_o, recip_o, et_o, stat_o,
    tok, wbuf, pt, lt, et, top, tot, pre, hid, slope, tbuf, part, rbuf, sbuf, send, recv, lsem,
):
    at = Place()
    cps = Copies(send, recv)
    rows, depth = tok.shape
    kk = lt.shape[1]
    peers = [at.X, at.YP, at.YM, at.CO] + [at.proto_peer(d) for d in range(1, 8)]
    greet(peers)
    me = at.slot(False, 0)
    load_pt = pltpu.make_async_copy(proto_t, pt, lsem.at[1])
    load_pt.start()
    own = pltpu.make_async_copy(w_in, wbuf.at[me], lsem.at[0])
    own.start()
    load_tok = pltpu.make_async_copy(tokens, tok, lsem.at[2])
    load_tok.start()
    t = teacher[...].astype(f32)
    tbuf[at.p] = (t * lax.rsqrt(jnp.sum(t * t, axis=1, keepdims=True) + norm_eps)).astype(bf16)
    met(len(peers))
    halves = [
        gather_rows(cps, at, w_in, wbuf, 0, 128, 80, 64, 32),
        gather_rows(cps, at, w_in, wbuf, 128, 128, 64, 64, 32),
    ]

    def advance():
        return list(zip(*[next(g) for g in halves]))

    def accumulate(landed):
        block = wbuf.shape[1] * 2
        for (one, chip), (two, _) in landed:
            one.wait_recv()
            two.wait_recv()
            lhs = tok[:, pl.ds(pl.multiple_of(chip * block, block), block)]

            def tile(j, _):
                cols = pl.ds(pl.multiple_of(j * 256, 256), 256)
                rhs = wbuf[pl.ds(chip * 2, 2), :, cols].reshape(block, 256)
                pre[:, cols] += jnp.dot(lhs, rhs, preferred_element_type=f32)
                return 0

            lax.fori_loop(0, pre.shape[1] // 256, tile, 0)

    started = advance()
    tc = [cps.start(tbuf.at[at.p], tbuf.at[at.p], at.proto_peer(d)) for d in range(1, 8)]
    pre[...] = jnp.zeros_like(pre)
    load_pt.wait()
    for k in tc:
        k.wait_recv()
    tn = tbuf[...].reshape(rows, tbuf.shape[2])
    step = 512

    def score(j, best):
        cols = pl.ds(pl.multiple_of(j * step, step), step)
        v = jnp.dot(tn, pt[:, cols], preferred_element_type=f32)
        v = (v - center[:, cols]) * (1.0 / tau_teacher)
        lt[:, cols] = v
        for q in range(step // 128):
            best = jnp.maximum(best, v[:, q * 128 : (q + 1) * 128])
        return best

    top[...] = lax.fori_loop(0, kk // step, score, jnp.full((rows, 128), -jnp.inf, f32))
    own.wait()
    load_tok.wait()
    first = advance()
    top[...] = jnp.broadcast_to(jnp.max(top[...], axis=1, keepdims=True), (rows, 128))
    tot[...] = jnp.zeros_like(tot)

    def lift(j, _):
        cols = pl.ds(pl.multiple_of(j * 128, 128), 128)
        e = jnp.exp(lt[:, cols] - top[...])
        et[:, cols] = e.astype(bf16)
        tot[...] += e
        return 0

    lax.fori_loop(0, kk // 128, lift, 0)
    save = pltpu.make_async_copy(et, et_o, lsem.at[3])
    save.start()
    accumulate(started)
    second = advance()
    stat_o[...] = jnp.concatenate(
        [
            jnp.transpose(top[...])[0:1],
            jnp.sum(jnp.transpose(tot[...]), axis=0, keepdims=True),
            jnp.zeros((6, rows), f32),
        ],
        axis=0,
    )
    accumulate(first)
    third = advance()
    accumulate(second)
    accumulate(third)

    small = part.shape[1]

    def act(q):
        rs = pl.ds(pl.multiple_of(q * small, small), small)
        value, grade = gelu_parts(pre[rs, :])
        slope[rs, :] = grade
        h = value.astype(bf16)
        hid[rs, :] = h
        part[q] = jnp.dot(h, w_out[...], preferred_element_type=f32)

    base = len(cps.all)

    def act_send(i, _):
        q = (at.p + i + 1) % 8
        act(q)
        pltpu.make_async_remote_copy(
            src_ref=part.at[q],
            dst_ref=rbuf.at[i],
            send_sem=send.at[base + i],
            recv_sem=recv.at[base + i],
            device_id=(at.r, q),
            device_id_type=MESH,
        ).start()
        return 0

    lax.fori_loop(0, 7, act_send, 0)
    act(at.p)
    save_hid = pltpu.make_async_copy(hid, hid_o, lsem.at[4])
    save_hid.start()
    save_slope = pltpu.make_async_copy(slope, slope_o, lsem.at[5])
    save_slope.start()
    total = part[at.p]
    for i in range(7):
        cps.expect(rbuf.at[i], base + i, at.proto_peer(i + 1)).wait_recv()
        total = total + rbuf[i]
    recip = lax.rsqrt(jnp.sum(total * total, axis=1, keepdims=True) + norm_eps)
    unit = total * recip
    sbuf[at.p] = unit.astype(bf16)
    sc = [cps.start(sbuf.at[at.p], sbuf.at[at.p], at.proto_peer(d)) for d in range(1, 8)]
    unit_o[...] = unit
    recip_o[...] = jnp.broadcast_to(recip, recip_o.shape)
    for k in sc:
        k.wait_recv()
    sn_o[...] = sbuf[...].reshape(rows, sbuf.shape[2])
    save.wait()
    save_hid.wait()
    save_slope.wait()
    cps.finish()


def head(tokens, w_in, w_out, teacher_z, proto_teacher, center):
    rows, depth = tokens.shape
    hidden = w_in.shape[1]
    wide = w_out.shape[1]
    kk = proto_teacher.shape[1]
    small = teacher_z.shape[0]
    shp = jax.ShapeDtypeStruct
    copies = 40 + 7 + 7 + 7
    return pl.pallas_call(
        head_kernel,
        out_shape=(
            shp((rows, hidden), bf16), shp((rows, hidden), f32), shp((rows, wide), bf16),
            shp((small, wide), f32), shp((small, 128), f32), shp((rows, kk), bf16), shp((8, rows), f32),
        ),
        in_specs=[aspec(), aspec(), vspec(), vspec(), aspec(), vspec()],
        out_specs=(aspec(), aspec(), vspec(), vspec(), vspec(), aspec(), vspec()),
        scratch_shapes=[
            VMEM((rows, depth), bf16), VMEM((16,) + w_in.shape, bf16),
            VMEM(proto_teacher.shape, bf16), VMEM((rows, kk), f32), VMEM((rows, kk), bf16),
            VMEM((rows, 128), f32), VMEM((rows, 128), f32),
            VMEM((rows, hidden), f32), VMEM((rows, hidden), bf16), VMEM((rows, hidden), f32),
            VMEM((8, small, wide), bf16), VMEM((8, small, wide), f32),
            VMEM((7, small, wide), f32), VMEM((8, small, wide), bf16),
            pltpu.SemaphoreType.DMA((copies,)), pltpu.SemaphoreType.DMA((copies,)),
            pltpu.SemaphoreType.DMA((6,)),
        ],
        compiler_params=pltpu.CompilerParams(
            collective_id=0, has_side_effects=True, vmem_limit_bytes=62 * 2**20
        ),
        name="head",
    )(tokens, w_in, w_out, teacher_z, proto_teacher, center[None, :])


def along(col):
    return jnp.transpose(col)


def middle_kernel(
    sn, proto_s, et_in, stat_t, image, unit, recip,
    dbott_o, pgrad_o, loss_o,
    ps, et, ls, gs, snt, ms, ss, cs, cbuf, stats, fsb, ftb, S, snd, rc, far, nm, np_, xb, xa, fin, fcore,
    dacc, dpart, drecv, dbuf, send, recv, lsem,
):
    at = Place()
    cps = Copies(send, recv)
    rows, kk = ls.shape
    half = kk // 2
    peers = [at.proto_peer(d) for d in range(1, 8)] + [at.row_peer(d) for d in range(1, 16)]
    greet(peers)
    load_ps = pltpu.make_async_copy(proto_s, ps, lsem.at[0])
    load_ps.start()
    load_et = pltpu.make_async_copy(et_in, et, lsem.at[1])
    load_et.start()
    snt[...] = jnp.transpose(sn[...])
    images = cbuf.shape[1]
    onehot = (lax.broadcasted_iota(jnp.int32, (images, rows), 0) == image[...]).astype(f32)
    cbuf[at.r] = jnp.broadcast_to(jnp.sum(onehot, axis=1, keepdims=True), cbuf.shape[1:])
    load_ps.wait()
    step = 512

    def one(j, top):
        cols = pl.ds(pl.multiple_of(j * step, step), step)
        v = jnp.dot(sn[...], ps[:, cols], preferred_element_type=f32) * (1.0 / tau_student)
        ls[:, cols] = v
        for q in range(step // 128):
            top = jnp.maximum(top, v[:, q * 128 : (q + 1) * 128])
        return top

    ms[...] = lax.fori_loop(0, kk // step, one, jnp.full((rows, 128), -jnp.inf, f32))
    met(len(peers))
    cc = [cps.start(cbuf.at[at.r], cbuf.at[at.r], at.row_peer(d)) for d in range(1, 16)]
    ms[...] = jnp.broadcast_to(jnp.max(ms[...], axis=1, keepdims=True), (rows, 128))
    ss[...] = jnp.zeros_like(ss)
    cs[...] = jnp.zeros_like(cs)
    load_et.wait()

    def two(j, _):
        cols = pl.ds(pl.multiple_of(j * 128, 128), 128)
        d = ls[:, cols] - ms[...]
        e = jnp.exp(d)
        ls[:, cols] = e
        ss[...] += e
        cs[...] += et[:, cols].astype(f32) * d
        return 0

    lax.fori_loop(0, kk // 128, two, 0)
    stats[at.p] = jnp.concatenate(
        [
            stat_t[0:2],
            along(ms[...])[0:1],
            jnp.sum(along(ss[...]), axis=0, keepdims=True),
            jnp.sum(along(cs[...]), axis=0, keepdims=True),
            jnp.zeros((3, rows), f32),
        ],
        axis=0,
    )
    sc = [cps.start(stats.at[at.p], stats.at[at.p], at.proto_peer(d)) for d in range(1, 8)]
    for k in cc:
        k.wait_recv()
    counts = jnp.sum(cbuf[...], axis=0)[:, 0:1]
    w_row = 1.0 / (images * jnp.sum(onehot * counts, axis=0, keepdims=True))
    for k in sc:
        k.wait_recv()
    table = [stats[q] for q in range(8)]
    top_t = table[0][0:1]
    top_s = table[0][2:3]
    for q in table[1:]:
        top_t = jnp.maximum(top_t, q[0:1])
        top_s = jnp.maximum(top_s, q[2:3])
    total_t = total_s = cross = jnp.zeros((1, rows), f32)
    for q in table:
        scale = jnp.exp(q[0:1] - top_t)
        total_t = total_t + q[1:2] * scale
        total_s = total_s + q[3:4] * jnp.exp(q[2:3] - top_s)
        cross = cross + scale * (q[4:5] + q[1:2] * (q[2:3] - top_s))
    cross = jnp.log(total_s) - cross / total_t
    loss_o[...] = jnp.broadcast_to(w_row * cross, loss_o.shape)
    mine = stats[at.p]
    lift = (loss_scale / tau_student) * w_row
    fsb[...] = across(lift * jnp.exp(mine[2:3] - top_s) / total_s)
    ftb[...] = across(lift * jnp.exp(mine[0:1] - top_t) / total_t)
    dacc[...] = jnp.zeros_like(dacc)

    def grads(base, dst):
        def one(j, _):
            first = base + j * step
            for q in range(step // 128):
                cols = pl.ds(pl.multiple_of(first + q * 128, 128), 128)
                v = ls[:, cols] * fsb[...] - et[:, cols].astype(f32) * ftb[...]
                gs[:, q * 128 : (q + 1) * 128] = v.astype(bf16)
            cols = pl.ds(pl.multiple_of(first, step), step)
            g = gs[...]
            v = jnp.dot(snt[...], g, preferred_element_type=f32)
            dst[:, :, pl.ds(pl.multiple_of(j * step, step), step)] = v.astype(bf16).reshape(
                dst.shape[0], dst.shape[1], step
            )
            d = lax.dot_general(
                g, ps[:, cols], (((1,), (1,)), ((), ())), preferred_element_type=f32
            )
            dacc[...] += d
            return 0

        lax.fori_loop(0, half // step, one, 0)

    grads((1 - at.c) * half, snd)
    swap = cps.start(snd, rc, at.CO)
    grads(at.c * half, S)
    dpart[...] = dacc[...].astype(bf16).reshape(dpart.shape)
    dc = [
        cps.start(dpart.at[(at.p + d) % 8], drecv.at[d], at.proto_peer(d)) for d in range(1, 8)
    ]
    swap.wait_recv()
    rs = Scatter(cps, at, S, (far, nm, np_, xb, xa), 1, 1792, 768, 640)
    for other, dy in ORDER:
        g = at.chip(other, dy)
        S[g] = (S[g].astype(f32) + rc[g].astype(f32)).astype(bf16)
        rs.ready(other, dy)
    total = dpart[at.p].astype(f32)
    for d in range(1, 8):
        dc[d - 1].wait_recv()
        total = total + drecv[d].astype(f32)
    u, r = unit[...], recip[:, 0:1]
    dbuf[at.p] = (r * (total - u * jnp.sum(u * total, axis=1, keepdims=True))).astype(bf16)
    bc = [cps.start(dbuf.at[at.p], dbuf.at[at.p], at.proto_peer(d)) for d in range(1, 8)]
    for dy in (2, 1, 3, 0):
        rs.ready_x(dy)
    rs.mid_a(1)
    rs.mid_a(0)
    rs.late_a()
    rs.mid_b()
    rs.late_b()
    for k in bc:
        k.wait_recv()
    dbott_o[...] = dbuf[...].reshape(dbott_o.shape)
    rs.final(fin)
    n = fcore.shape[0]
    keep, give = at.c * n, (1 - at.c) * n
    fc = cps.start(fin.at[pl.ds(pl.multiple_of(give, 8), n)], fcore, at.CO)
    pgrad_o[:, pl.ds(pl.multiple_of(at.c * half, half), half)] = fin[pl.ds(pl.multiple_of(keep, 8), n), :]
    fc.wait_recv()
    pgrad_o[:, pl.ds(pl.multiple_of((1 - at.c) * half, half), half)] = fcore[...]
    cps.finish()


def middle(sn, proto_s, et, stat_t, image, unit, recip):
    rows, wide = sn.shape
    kk = proto_s.shape[1]
    small = unit.shape[0]
    shp = jax.ShapeDtypeStruct
    chunk = (wide // 8, kk // 2)
    copies = 15 + 7 + 1 + 7 + 7 + 23 + 1
    lane = VMEM((rows, 128), f32)
    return pl.pallas_call(
        middle_kernel,
        out_shape=(shp((rows, wide), bf16), shp((wide // 16, kk), f32), shp((8, rows), f32)),
        in_specs=[vspec(), aspec(), aspec()] + [vspec()] * 4,
        out_specs=(vspec(),) * 3,
        scratch_shapes=[
            VMEM((wide, kk), bf16), VMEM((rows, kk), bf16), VMEM((rows, kk), f32), VMEM((rows, 512), bf16),
            VMEM((wide, rows), bf16), lane, lane, lane, VMEM((16, 64, 128), f32), VMEM((8, 8, rows), f32), lane, lane,
            VMEM((8,) + chunk, bf16), VMEM((8,) + chunk, bf16), VMEM((8,) + chunk, bf16),
            *scatter_bufs(chunk), VMEM(chunk, f32), VMEM((chunk[0] // 2, chunk[1]), f32),
            VMEM((rows, wide), f32), VMEM((8, small, wide), bf16), VMEM((8, small, wide), bf16), VMEM((8, small, wide), bf16),
            pltpu.SemaphoreType.DMA((copies,)), pltpu.SemaphoreType.DMA((copies,)),
            pltpu.SemaphoreType.DMA((2,)),
        ],
        compiler_params=pltpu.CompilerParams(
            collective_id=1, has_side_effects=True, vmem_limit_bytes=62 * 2**20
        ),
        name="middle",
    )(sn, proto_s, et, stat_t, image, unit, recip)


def tail_kernel(
    tokens, hid_in, slope_in, dbott, w_out, loss_in,
    wgrad_o, wout_o, loss_o,
    tok, hid, slope, dp, S, snd, rc, far, nm, np_, xb, xa, fin, fcore,
    W, S2, rc2, far2, nm2, np2, xb2, xa2, fin2, own2, wbuf, lbuf, send, recv, lsem,
):
    at = Place()
    cps = Copies(send, recv)
    rows, hidden = dp.shape
    half = hidden // 2
    peers = [at.row_peer(d) for d in range(1, 16)]
    greet(peers)
    load_tok = pltpu.make_async_copy(tokens, tok, lsem.at[0])
    load_tok.start()
    load_hid = pltpu.make_async_copy(hid_in, hid, lsem.at[2])
    load_hid.start()
    load_slope = pltpu.make_async_copy(slope_in, slope, lsem.at[1])
    load_slope.start()
    lbuf[at.r] = jnp.broadcast_to(
        jnp.sum(loss_in[...], axis=1, keepdims=True), lbuf.shape[1:]
    )
    load_slope.wait()

    def back(j, _):
        cols = pl.ds(pl.multiple_of(j * 256, 256), 256)
        v = lax.dot_general(
            dbott[...], w_out[cols, :], (((1,), (1,)), ((), ())), preferred_element_type=f32
        )
        dp[:, cols] = (v * slope[:, cols]).astype(bf16)
        return 0

    lax.fori_loop(0, hidden // 256, back, 0)
    load_tok.wait()
    met(len(peers))
    rs = Scatter(cps, at, S, (far, nm, np_, xb, xa), 0, 288, 128, 112)
    rs2 = Scatter(cps, at, S2, (far2, nm2, np2, xb2, xa2), 0, 32, 16, 16)
    swaps = {}

    def chunk(other, dy):
        g = at.chip(other, dy)
        lhs = pl.ds(pl.multiple_of(g * 512, 512), 512)
        for dst, side in ((snd, 1 - at.c), (S, at.c)):
            rhs = pl.ds(pl.multiple_of(side * half, half), half)
            dst[g] = lax.dot_general(
                tok[:, lhs], dp[:, rhs], (((0,), (0,)), ((), ())), preferred_element_type=f32
            ).astype(bf16)
            if dst is snd:
                swaps[other, dy] = cps.start(snd.at[g], rc.at[g], at.CO)

    def merge(other, dy):
        g = at.chip(other, dy)
        swaps[other, dy].wait_recv()
        S[g] = (S[g].astype(f32) + rc[g].astype(f32)).astype(bf16)
        rs.ready(other, dy)
        if other:
            rs.ready_x(dy)

    def out_grad():
        load_hid.wait()
        small = W.shape[2]
        for j in range(hidden // 256):
            cols = slice(j * 256, (j + 1) * 256)
            v = lax.dot_general(
                hid[:, cols], dbott[...], (((0,), (0,)), ((), ())), preferred_element_type=f32
            ).astype(bf16)
            for i in range(256 // small):
                k = j * (256 // small) + i
                W[k % 2, k // 2] = v[i * small : (i + 1) * small]
        loss_c = [cps.start(lbuf.at[at.r], lbuf.at[at.r], at.row_peer(d)) for d in range(1, 16)]
        swap = cps.start(W.at[1 - at.c], rc2, at.CO)
        return loss_c, swap

    for i, key in enumerate(ORDER):
        chunk(*key)
        if i > 0:
            merge(*ORDER[i - 1])
        if i == 1:
            lc, swap2 = out_grad()
        if i == 2:
            swap2.wait_recv()
            S2[...] = (W[at.c].astype(f32) + rc2[...].astype(f32)).astype(bf16)
            for k2 in ORDER:
                rs2.ready(*k2)
                if k2[0]:
                    rs2.ready_x(k2[1])
        if i == 4:
            rs2.mid_a(1)
            rs2.mid_b()
            rs2.mid_a(0)
        if i == 5:
            rs.mid_a(1)
        if i == 6:
            rs2.late_a()
            rs2.late_b()
    merge(*ORDER[-1])
    rs2.final(fin2)
    own2[...] = fin2[...].astype(bf16)
    wbuf[at.r] = own2[...]
    gather = gather_rows(cps, at, own2, wbuf, 0, 64, 32, 32, 16)
    landed = list(next(gather))
    rs.mid_b()
    rs.mid_a(0)
    landed += next(gather)
    rs.late_a()
    landed += next(gather)
    rs.late_b()
    landed += next(gather)
    rs.final(fin)
    n = fcore.shape[0]
    fc = cps.start(fin.at[pl.ds(pl.multiple_of((1 - at.c) * n, n), n)], fcore, at.CO)
    wgrad_o[:, pl.ds(pl.multiple_of(at.c * half, half), half)] = fin[pl.ds(pl.multiple_of(at.c * n, n), n), :]
    for copy, _ in landed:
        copy.wait_recv()
    wout_o[...] = wbuf[...].reshape(wout_o.shape)
    for k in lc:
        k.wait_recv()
    loss_o[...] = jnp.sum(lbuf[...], axis=0)
    fc.wait_recv()
    wgrad_o[:, pl.ds(pl.multiple_of((1 - at.c) * half, half), half)] = fcore[...]
    cps.finish()


def tail(tokens, hid, slope, dbott, w_out, loss_row):
    rows, depth = tokens.shape
    hidden, wide = w_out.shape
    shp = jax.ShapeDtypeStruct
    block = (depth // 8, hidden // 2)
    small = (hidden // 16, wide)
    copies = 15 + 1 + 8 + 23 + 23 + 20 + 1
    return pl.pallas_call(
        tail_kernel,
        out_shape=(shp((depth // 16, hidden), f32), shp((hidden, wide), bf16), shp((8, 128), f32)),
        in_specs=[aspec(), aspec(), aspec(), vspec(), vspec(), vspec()],
        out_specs=(vspec(),) * 3,
        scratch_shapes=[
            VMEM((rows, depth), bf16), VMEM((rows, hidden), bf16), VMEM((rows, hidden), f32), VMEM((rows, hidden), bf16),
            VMEM((8,) + block, bf16), VMEM((8,) + block, bf16), VMEM((8,) + block, bf16),
            *scatter_bufs(block), VMEM(block, f32), VMEM((block[0] // 2, block[1]), f32),
            VMEM((2, 8) + small, bf16), VMEM((8,) + small, bf16), VMEM((8,) + small, bf16),
            *scatter_bufs(small), VMEM(small, f32), VMEM(small, bf16), VMEM((16,) + small, bf16),
            VMEM((16, 8, 128), f32),
            pltpu.SemaphoreType.DMA((copies,)), pltpu.SemaphoreType.DMA((copies,)),
            pltpu.SemaphoreType.DMA((3,)),
        ],
        compiler_params=pltpu.CompilerParams(
            collective_id=2, has_side_effects=True, vmem_limit_bytes=62 * 2**20
        ),
        name="tail",
    )(tokens, hid, slope, dbott, w_out, loss_row)


def close_kernel(wg, wo, pg, loss, wg_o, wo_o, pg_o, loss_o):
    wg_o[...] = wg[...]
    wo_o[...] = wo[...].astype(f32)
    pg_o[...] = pg[...]
    loss_o[0, 0] = loss[0, 0]


def close(wg, wo, pg, loss):
    shp = jax.ShapeDtypeStruct
    n = 2
    specs = [
        pl.BlockSpec((wg.shape[0] // n, wg.shape[1]), lambda i: (i, 0)),
        pl.BlockSpec((wo.shape[0] // n, wo.shape[1]), lambda i: (i, 0)),
        pl.BlockSpec((pg.shape[0], pg.shape[1] // n), lambda i: (0, i)),
    ]
    return pl.pallas_call(
        close_kernel,
        grid=(n,),
        out_shape=(shp(wg.shape, f32), shp(wo.shape, f32), shp(pg.shape, f32), shp((1, 1), f32)),
        in_specs=specs + [pl.BlockSpec((8, 128), lambda i: (0, 0))],
        out_specs=tuple(specs) + (pl.BlockSpec((1, 1), lambda i: (0, 0), memory_space=pltpu.SMEM),),
        name="close",
    )(wg, wo, pg, loss)


def on_device(tokens, w_in, w_out, teacher_z, proto_student, proto_teacher, center, image_of):
    hidden, slope, student_n, unit, recip, exp_t, stat_t = head(
        tokens, w_in, w_out, teacher_z, proto_teacher, center
    )
    dbott, proto_grad, loss_row = middle(
        student_n, proto_student, exp_t, stat_t, image_of[None, :], unit, recip
    )
    w_in_grad, w_out_grad, loss = tail(tokens, hidden, slope, dbott, w_out, loss_row)
    w_in_grad, w_out_grad, proto_grad, loss = close(w_in_grad, w_out_grad, proto_grad, loss)
    return (loss[0, 0], w_in_grad, w_out_grad, proto_grad)


def solution(mesh):
    return jax.shard_map(
        on_device,
        mesh=mesh,
        in_specs=(
            P("row", None),
            P("row", "proto"),
            P("proto", None),
            P(("row", "proto"), None),
            P(None, "proto"),
            P(None, "proto"),
            P("proto"),
            P("row"),
        ),
        out_specs=(P(), P("row", "proto"), P("proto", None), P("row", "proto")),
        check_vma=False,
    )
```

time: 214 us -> 197 us (0.921)
  local copies, waits for them, and re-layouts: 8.54 us -> 0 us
  Pallas kernels: 204 us -> 196 us
    pallas_call x1 -> x2, Pallas kernels: 83.7 us -> 74.8 us  [the longest x1 71.7 us: head(): pl.pallas_call(head_kernel, out_shape=(shp((rows, hidden), bf16), shp((ro...]
    unnamed x5 -> x0, local copies, waits for them, and re-layouts: 5.78 us -> none
    pallas_call x1, Pallas kernels: 55.7 us -> 58.4 us  [tail(): pl.pallas_call(tail_kernel, out_shape=(shp((depth // 16, hidden), f32), s...]
where the time goes in v3:
time: 197 us
  Pallas kernels  196 us (99%)
    pallas_call x1, Pallas kernels, head(): pl.pallas_call(head_kernel, out_shape=(shp((rows, hidden), bf16), shp((ro...  71.7 us
    pallas_call x1, Pallas kernels, middle(): pl.pallas_call(middle_kernel, out_shape=(shp((rows, wide), bf16), shp((wi...  63.1 us
    pallas_call x1, Pallas kernels, tail(): pl.pallas_call(tail_kernel, out_shape=(shp((depth // 16, hidden), f32), s...  58.4 us

profile of v3, /device:TPU:1, one launch (start us, length us, event | category | flops | bytes accessed | tf_op | source)
XLA Modules:
  0.0 196.9 jit_solution(7447185532209544494)
XLA Ops:
  0.6 71.7 %head.1 = (bf16[512,1024]{1,0:T(8,128)(2,1)}, f32[512,1024]{1,0:T(8,128)}, bf16[512,384]{1,0:T(8,128)(2,1)}, f32[64,384]{1,0:T(8,128)}, f32[64,128]{1,0:T(8,128)...) custom-call(bf16[512,4096]{1,0:T(8,128)(2,1)} %tokens.3, bf16[256,1024]{1,0:T(8,128)(2,1)} %w_in.1, ...), custom_call_target="tpu_custom_call" | custom-call | tf_op jit(solution)/shard_map/head/pallas_call | solution.py:427
  72.4 63.1 %middle.1 = (bf16[512,384]{1,0:T(8,128)(2,1)}, f32[24,6144]{1,0:T(8,128)}, f32[8,512]{1,0:T(8,128)}) custom-call(bf16[512,384]{1,0:T(8,128)(2,1)} %get-tuple-element.23.sn, bf16[384,6144]{1,0:T(8,128)(2,1)} %proto_s.1, bf16[512,6144]{1,0:T(8,128)(2,1)} %get-tuple-element.24.et_in, f32[8,512]{1,0:T(8,128)} %get-tuple-element.25.stat_t, s32[1,512]{1,0:T(1,128)} %bitcast.4, ...), custom_call_target="tpu_custom_call" | custom-call | tf_op jit(solution)/shard_map/middle/pallas_call | solution.py:611
  135.4 58.4 %tail.1 = (f32[256,1024]{1,0:T(8,128)}, bf16[1024,384]{1,0:T(8,128)(2,1)}, f32[8,128]{1,0:T(8,128)}) custom-call(bf16[512,4096]{1,0:T(8,128)(2,1)} %tokens.3, bf16[512,1024]{1,0:T(8,128)(2,1)} %get-tuple-element.21.hid_in, f32[512,1024]{1,0:T(8,128)} %get-tuple-element.22.slope_in, bf16[512,384]{1,0:T(8,128)(2,1)} %get-tuple-element.28.dbott, ...), custom_call_target="tpu_custom_call" | custom-call | tf_op jit(solution)/shard_map/tail/pallas_call | solution.py:761
  193.9 3.1 %close.1 = (f32[256,1024]{1,0:T(8,128)}, f32[1024,384]{1,0:T(8,128)}, f32[24,6144]{1,0:T(8,128)}, f32[1,1]{1,0:T(1,128)}) custom-call(f32[256,1024]{1,0:T(8,128)} %get-tuple-element.30.wg, bf16[1024,384]{1,0:T(8,128)(2,1)} %get-tuple-element.31.wo, f32[24,6144]{1,0:T(8,128)} %get-tuple-element.32.pg, f32[8,128]{1,0:T(8,128)} %get-tuple-element.33.loss), custom_call_target="tpu_custom_call" | custom-call | tf_op jit(solution)/shard_map/close/pallas_call | solution.py:798

commit v4 on v3

--- a/solution.py
+++ b/solution.py
@@ -223,18 +223,17 @@
         self.add(g3, self.Alo, (self.far, k))
         self.send(("pl", k), g3, self.np, k, self.Alo, self.at.YM)
 
-    def mid_b(self):
-        for dy in (2, 1, 3):
-            g = self.at.chip(False, dy)
-            self.wait(("x", dy))
-            self.add(g, self.B, (self.xb, dy))
-            if dy == 2:
-                self.send("bfu", g, self.far, 0, self.Bup, self.at.YP)
-                self.send("bfl", g, self.far, 0, self.Blo, self.at.YM)
-            elif dy == 1:
-                self.send("bml", g, self.nm, 0, self.Blo, self.at.YP)
-            else:
-                self.send("bpu", g, self.np, 0, self.Bup, self.at.YM)
+    def mid_b(self, dy):
+        g = self.at.chip(False, dy)
+        self.wait(("x", dy))
+        self.add(g, self.B, (self.xb, dy))
+        if dy == 2:
+            self.send("bfu", g, self.far, 0, self.Bup, self.at.YP)
+            self.send("bfl", g, self.far, 0, self.Blo, self.at.YM)
+        elif dy == 1:
+            self.send("bml", g, self.nm, 0, self.Blo, self.at.YP)
+        else:
+            self.send("bpu", g, self.np, 0, self.Bup, self.at.YM)
 
     def late_a(self):
         for key in ("ml", "mu", "pl", "pu"):
@@ -316,8 +315,8 @@
 
             lax.fori_loop(0, pre.shape[1] // 256, tile, 0)
 
+    tc = [cps.start(tbuf.at[at.p], tbuf.at[at.p], at.proto_peer(d)) for d in range(1, 8)]
     started = advance()
-    tc = [cps.start(tbuf.at[at.p], tbuf.at[at.p], at.proto_peer(d)) for d in range(1, 8)]
     pre[...] = jnp.zeros_like(pre)
     load_pt.wait()
     for k in tc:
@@ -339,16 +338,23 @@
     load_tok.wait()
     first = advance()
     top[...] = jnp.broadcast_to(jnp.max(top[...], axis=1, keepdims=True), (rows, 128))
-    tot[...] = jnp.zeros_like(tot)
-
-    def lift(j, _):
-        cols = pl.ds(pl.multiple_of(j * 128, 128), 128)
-        e = jnp.exp(lt[:, cols] - top[...])
-        et[:, cols] = e.astype(bf16)
-        tot[...] += e
+
+    def lift(i, _):
+        rs = pl.ds(pl.multiple_of(i * 64, 64), 64)
+        peak = top[rs, :]
+
+        def tile(j, acc):
+            for q in range(4):
+                cols = pl.ds(pl.multiple_of(j * 512 + q * 128, 128), 128)
+                e = jnp.exp(lt[rs, cols] - peak)
+                et[rs, cols] = e.astype(bf16)
+                acc = acc + e
+            return acc
+
+        tot[rs, :] = lax.fori_loop(0, kk // 512, tile, jnp.zeros((64, 128), f32))
         return 0
 
-    lax.fori_loop(0, kk // 128, lift, 0)
+    lax.fori_loop(0, rows // 64, lift, 0)
     save = pltpu.make_async_copy(et, et_o, lsem.at[3])
     save.start()
     accumulate(started)
@@ -362,8 +368,8 @@
         axis=0,
     )
     accumulate(first)
+    accumulate(second)
     third = advance()
-    accumulate(second)
     accumulate(third)
 
     small = part.shape[1]
@@ -456,7 +462,9 @@
 def middle_kernel(
     sn, proto_s, et_in, stat_t, image, unit, recip,
     dbott_o, pgrad_o, loss_o,
-    ps, et, ls, gs, snt, ms, ss, cs, cbuf, stats, fsb, ftb, S, snd, rc, far, nm, np_, xb, xa, fin, fcore,
+    ps, et, ls, gs, snt, ms, ss, cs, cbuf, stats, fsb, ftb,
+    S, snd, rc, far, nm, np_, xb, xa, fin, fcore,
+    S_, snd_, rc_, far_, nm_, np__, xb_, xa_, fin_, fcore_,
     dacc, dpart, drecv, dbuf, send, recv, lsem,
 ):
     at = Place()
@@ -488,20 +496,28 @@
     met(len(peers))
     cc = [cps.start(cbuf.at[at.r], cbuf.at[at.r], at.row_peer(d)) for d in range(1, 16)]
     ms[...] = jnp.broadcast_to(jnp.max(ms[...], axis=1, keepdims=True), (rows, 128))
-    ss[...] = jnp.zeros_like(ss)
-    cs[...] = jnp.zeros_like(cs)
     load_et.wait()
 
-    def two(j, _):
-        cols = pl.ds(pl.multiple_of(j * 128, 128), 128)
-        d = ls[:, cols] - ms[...]
-        e = jnp.exp(d)
-        ls[:, cols] = e
-        ss[...] += e
-        cs[...] += et[:, cols].astype(f32) * d
+    def two(i, _):
+        rs = pl.ds(pl.multiple_of(i * 64, 64), 64)
+        peak = ms[rs, :]
+
+        def tile(j, acc):
+            s, c = acc
+            for q in range(4):
+                cols = pl.ds(pl.multiple_of(j * 512 + q * 128, 128), 128)
+                d = ls[rs, cols] - peak
+                e = jnp.exp(d)
+                ls[rs, cols] = e
+                s = s + e
+                c = c + et[rs, cols].astype(f32) * d
+            return s, c
+
+        zero = jnp.zeros((64, 128), f32)
+        ss[rs, :], cs[rs, :] = lax.fori_loop(0, kk // 512, tile, (zero, zero))
         return 0
 
-    lax.fori_loop(0, kk // 128, two, 0)
+    lax.fori_loop(0, rows // 64, two, 0)
     stats[at.p] = jnp.concatenate(
         [
             stat_t[0:2],
@@ -542,10 +558,17 @@
     def grads(base, dst):
         def one(j, _):
             first = base + j * step
-            for q in range(step // 128):
-                cols = pl.ds(pl.multiple_of(first + q * 128, 128), 128)
-                v = ls[:, cols] * fsb[...] - et[:, cols].astype(f32) * ftb[...]
-                gs[:, q * 128 : (q + 1) * 128] = v.astype(bf16)
+
+            def block(i, _):
+                rs = pl.ds(pl.multiple_of(i * 64, 64), 64)
+                f_s, f_t = fsb[rs, :], ftb[rs, :]
+                for q in range(step // 128):
+                    cols = pl.ds(pl.multiple_of(first + q * 128, 128), 128)
+                    v = ls[rs, cols] * f_s - et[rs, cols].astype(f32) * f_t
+                    gs[rs, q * 128 : (q + 1) * 128] = v.astype(bf16)
+                return 0
+
+            lax.fori_loop(0, rows // 64, block, 0)
             cols = pl.ds(pl.multiple_of(first, step), step)
             g = gs[...]
             v = jnp.dot(snt[...], g, preferred_element_type=f32)
@@ -558,21 +581,37 @@
             dacc[...] += d
             return 0
 
-        lax.fori_loop(0, half // step, one, 0)
-
-    grads((1 - at.c) * half, snd)
+        lax.fori_loop(0, dst.shape[2] // step, one, 0)
+
+    quarter = half // 2
+    mine_at, other_at = at.c * half, (1 - at.c) * half
+    one = Scatter(cps, at, S, (far, nm, np_, xb, xa), 1, 896, 384, 256)
+    two = Scatter(cps, at, S_, (far_, nm_, np__, xb_, xa_), 1, 896, 512, 384)
+
+    def merge(rs, S, rc, swap):
+        swap.wait_recv()
+        for other, dy in ORDER:
+            g = at.chip(other, dy)
+            S[g] = (S[g].astype(f32) + rc[g].astype(f32)).astype(bf16)
+            rs.ready(other, dy)
+            if other:
+                rs.ready_x(dy)
+
+    grads(other_at, snd)
     swap = cps.start(snd, rc, at.CO)
-    grads(at.c * half, S)
+    grads(mine_at, S)
+    grads(other_at + quarter, snd_)
+    swap_ = cps.start(snd_, rc_, at.CO)
+    merge(one, S, rc, swap)
+    grads(mine_at + quarter, S_)
     dpart[...] = dacc[...].astype(bf16).reshape(dpart.shape)
     dc = [
         cps.start(dpart.at[(at.p + d) % 8], drecv.at[d], at.proto_peer(d)) for d in range(1, 8)
     ]
-    swap.wait_recv()
-    rs = Scatter(cps, at, S, (far, nm, np_, xb, xa), 1, 1792, 768, 640)
-    for other, dy in ORDER:
-        g = at.chip(other, dy)
-        S[g] = (S[g].astype(f32) + rc[g].astype(f32)).astype(bf16)
-        rs.ready(other, dy)
+    one.mid_a(1)
+    merge(two, S_, rc_, swap_)
+    one.mid_b(2)
+    one.mid_a(0)
     total = dpart[at.p].astype(f32)
     for d in range(1, 8):
         dc[d - 1].wait_recv()
@@ -580,23 +619,35 @@
     u, r = unit[...], recip[:, 0:1]
     dbuf[at.p] = (r * (total - u * jnp.sum(u * total, axis=1, keepdims=True))).astype(bf16)
     bc = [cps.start(dbuf.at[at.p], dbuf.at[at.p], at.proto_peer(d)) for d in range(1, 8)]
-    for dy in (2, 1, 3, 0):
-        rs.ready_x(dy)
-    rs.mid_a(1)
-    rs.mid_a(0)
-    rs.late_a()
-    rs.mid_b()
-    rs.late_b()
+    one.mid_b(1)
+    one.late_a()
+    one.mid_b(3)
+    two.mid_a(1)
+    one.late_b()
+    two.mid_b(2)
+    two.mid_a(0)
+    two.mid_b(1)
+    two.late_a()
+    two.mid_b(3)
+    two.late_b()
+    n = fcore.shape[0]
+    keep, give = pl.ds(pl.multiple_of(at.c * n, 8), n), pl.ds(pl.multiple_of((1 - at.c) * n, 8), n)
+
+    def settle(rs, fin, fcore, where):
+        rs.final(fin)
+        fc = cps.start(fin.at[give], fcore, at.CO)
+        pgrad_o[:, pl.ds(pl.multiple_of(mine_at + where, quarter), quarter)] = fin[keep, :]
+        return fc
+
+    fc = settle(one, fin, fcore, 0)
     for k in bc:
         k.wait_recv()
     dbott_o[...] = dbuf[...].reshape(dbott_o.shape)
-    rs.final(fin)
-    n = fcore.shape[0]
-    keep, give = at.c * n, (1 - at.c) * n
-    fc = cps.start(fin.at[pl.ds(pl.multiple_of(give, 8), n)], fcore, at.CO)
-    pgrad_o[:, pl.ds(pl.multiple_of(at.c * half, half), half)] = fin[pl.ds(pl.multiple_of(keep, 8), n), :]
+    fc_ = settle(two, fin_, fcore_, quarter)
     fc.wait_recv()
-    pgrad_o[:, pl.ds(pl.multiple_of((1 - at.c) * half, half), half)] = fcore[...]
+    pgrad_o[:, pl.ds(pl.multiple_of(other_at, half), quarter)] = fcore[...]
+    fc_.wait_recv()
+    pgrad_o[:, pl.ds(pl.multiple_of(other_at + quarter, quarter), quarter)] = fcore_[...]
     cps.finish()
 
 
@@ -605,9 +656,11 @@
     kk = proto_s.shape[1]
     small = unit.shape[0]
     shp = jax.ShapeDtypeStruct
-    chunk = (wide // 8, kk // 2)
-    copies = 15 + 7 + 1 + 7 + 7 + 23 + 1
+    chunk = (wide // 8, kk // 4)
+    copies = 15 + 7 + 7 + 7 + 2 * (1 + 23 + 1)
     lane = VMEM((rows, 128), f32)
+    part = [VMEM((8,) + chunk, bf16)] * 3 + scatter_bufs(chunk)
+    part += [VMEM(chunk, f32), VMEM((chunk[0] // 2, chunk[1]), f32)]
     return pl.pallas_call(
         middle_kernel,
         out_shape=(shp((rows, wide), bf16), shp((wide // 16, kk), f32), shp((8, rows), f32)),
@@ -616,8 +669,7 @@
         scratch_shapes=[
             VMEM((wide, kk), bf16), VMEM((rows, kk), bf16), VMEM((rows, kk), f32), VMEM((rows, 512), bf16),
             VMEM((wide, rows), bf16), lane, lane, lane, VMEM((16, 64, 128), f32), VMEM((8, 8, rows), f32), lane, lane,
-            VMEM((8,) + chunk, bf16), VMEM((8,) + chunk, bf16), VMEM((8,) + chunk, bf16),
-            *scatter_bufs(chunk), VMEM(chunk, f32), VMEM((chunk[0] // 2, chunk[1]), f32),
+            *(part + part),
             VMEM((rows, wide), f32), VMEM((8, small, wide), bf16), VMEM((8, small, wide), bf16), VMEM((8, small, wide), bf16),
             pltpu.SemaphoreType.DMA((copies,)), pltpu.SemaphoreType.DMA((copies,)),
             pltpu.SemaphoreType.DMA((2,)),
@@ -633,7 +685,7 @@
     tokens, hid_in, slope_in, dbott, w_out, loss_in,
     wgrad_o, wout_o, loss_o,
     tok, hid, slope, dp, S, snd, rc, far, nm, np_, xb, xa, fin, fcore,
-    W, S2, rc2, far2, nm2, np2, xb2, xa2, fin2, own2, wbuf, lbuf, send, recv, lsem,
+    W, S2, rc2, r2, own2, wbuf, lbuf, send, recv, lsem,
 ):
     at = Place()
     cps = Copies(send, recv)
@@ -650,6 +702,19 @@
     lbuf[at.r] = jnp.broadcast_to(
         jnp.sum(loss_in[...], axis=1, keepdims=True), lbuf.shape[1:]
     )
+    load_hid.wait()
+    small = W.shape[2]
+    for j in range(hidden // 256):
+        cols = slice(j * 256, (j + 1) * 256)
+        v = lax.dot_general(
+            hid[:, cols], dbott[...], (((0,), (0,)), ((), ())), preferred_element_type=f32
+        ).astype(bf16)
+        for i in range(256 // small):
+            k = j * (256 // small) + i
+            W[k % 2, k // 2] = v[i * small : (i + 1) * small]
+    met(len(peers))
+    swap2 = cps.start(W.at[1 - at.c], rc2, at.CO)
+    lc = [cps.start(lbuf.at[at.r], lbuf.at[at.r], at.row_peer(d)) for d in range(1, 16)]
     load_slope.wait()
 
     def back(j, _):
@@ -662,9 +727,7 @@
 
     lax.fori_loop(0, hidden // 256, back, 0)
     load_tok.wait()
-    met(len(peers))
     rs = Scatter(cps, at, S, (far, nm, np_, xb, xa), 0, 288, 128, 112)
-    rs2 = Scatter(cps, at, S2, (far2, nm2, np2, xb2, xa2), 0, 32, 16, 16)
     swaps = {}
 
     def chunk(other, dy):
@@ -686,61 +749,48 @@
         if other:
             rs.ready_x(dy)
 
-    def out_grad():
-        load_hid.wait()
-        small = W.shape[2]
-        for j in range(hidden // 256):
-            cols = slice(j * 256, (j + 1) * 256)
-            v = lax.dot_general(
-                hid[:, cols], dbott[...], (((0,), (0,)), ((), ())), preferred_element_type=f32
-            ).astype(bf16)
-            for i in range(256 // small):
-                k = j * (256 // small) + i
-                W[k % 2, k // 2] = v[i * small : (i + 1) * small]
-        loss_c = [cps.start(lbuf.at[at.r], lbuf.at[at.r], at.row_peer(d)) for d in range(1, 16)]
-        swap = cps.start(W.at[1 - at.c], rc2, at.CO)
-        return loss_c, swap
-
+    swap2.wait_recv()
+    S2[...] = (W[at.c].astype(f32) + rc2[...].astype(f32)).astype(bf16)
+    around = [k for k in ORDER if k != (False, 0)]
+    sums = [
+        cps.start(S2.at[at.chip(o, dy)], r2.at[k], at.dev(at.slot(o, dy)))
+        for k, (o, dy) in enumerate(around)
+    ]
+    spread = []
     for i, key in enumerate(ORDER):
         chunk(*key)
         if i > 0:
             merge(*ORDER[i - 1])
-        if i == 1:
-            lc, swap2 = out_grad()
-        if i == 2:
-            swap2.wait_recv()
-            S2[...] = (W[at.c].astype(f32) + rc2[...].astype(f32)).astype(bf16)
-            for k2 in ORDER:
-                rs2.ready(*k2)
-                if k2[0]:
-                    rs2.ready_x(k2[1])
         if i == 4:
-            rs2.mid_a(1)
-            rs2.mid_b()
-            rs2.mid_a(0)
-        if i == 5:
+            total = S2[at.chip(False, 0)].astype(f32)
+            for k, cp in enumerate(sums):
+                cp.wait_recv()
+                total = total + r2[k].astype(f32)
+            own2[...] = total.astype(bf16)
+            wbuf[at.r] = own2[...]
+            spread = [
+                cps.start(own2, wbuf.at[at.r], at.dev(at.slot(o, dy))) for o, dy in around
+            ]
+            spread.append(cps.start(own2, wbuf.at[at.r], at.CO))
+        if i == 6:
             rs.mid_a(1)
-        if i == 6:
-            rs2.late_a()
-            rs2.late_b()
+    rs.mid_b(2)
     merge(*ORDER[-1])
-    rs2.final(fin2)
-    own2[...] = fin2[...].astype(bf16)
-    wbuf[at.r] = own2[...]
-    gather = gather_rows(cps, at, own2, wbuf, 0, 64, 32, 32, 16)
-    landed = list(next(gather))
-    rs.mid_b()
     rs.mid_a(0)
-    landed += next(gather)
+    rs.mid_b(1)
     rs.late_a()
-    landed += next(gather)
+    rs.mid_b(3)
+    landed = [spread[-1]]
+    for (o, dy), cp in zip(around, spread):
+        cp.wait_recv()
+        ref = wbuf.at[at.slot(o, (4 - dy) % 4)]
+        landed.append(cps.start(ref, ref, at.CO))
     rs.late_b()
-    landed += next(gather)
     rs.final(fin)
     n = fcore.shape[0]
     fc = cps.start(fin.at[pl.ds(pl.multiple_of((1 - at.c) * n, n), n)], fcore, at.CO)
     wgrad_o[:, pl.ds(pl.multiple_of(at.c * half, half), half)] = fin[pl.ds(pl.multiple_of(at.c * n, n), n), :]
-    for copy, _ in landed:
+    for copy in landed:
         copy.wait_recv()
     wout_o[...] = wbuf[...].reshape(wout_o.shape)
     for k in lc:
@@ -757,7 +807,7 @@
     shp = jax.ShapeDtypeStruct
     block = (depth // 8, hidden // 2)
     small = (hidden // 16, wide)
-    copies = 15 + 1 + 8 + 23 + 23 + 20 + 1
+    copies = 15 + 1 + 8 + 23 + 7 + 8 + 7 + 1
     return pl.pallas_call(
         tail_kernel,
         out_shape=(shp((depth // 16, hidden), f32), shp((hidden, wide), bf16), shp((8, 128), f32)),
@@ -768,7 +818,7 @@
             VMEM((8,) + block, bf16), VMEM((8,) + block, bf16), VMEM((8,) + block, bf16),
             *scatter_bufs(block), VMEM(block, f32), VMEM((block[0] // 2, block[1]), f32),
             VMEM((2, 8) + small, bf16), VMEM((8,) + small, bf16), VMEM((8,) + small, bf16),
-            *scatter_bufs(small), VMEM(small, f32), VMEM(small, bf16), VMEM((16,) + small, bf16),
+            VMEM((7,) + small, bf16), VMEM(small, bf16), VMEM((16,) + small, bf16),
             VMEM((16, 8, 128), f32),
             pltpu.SemaphoreType.DMA((copies,)), pltpu.SemaphoreType.DMA((copies,)),
             pltpu.SemaphoreType.DMA((3,)),

time: 197 us -> 178 us (0.904)
  Pallas kernels: 196 us -> 177 us
    pallas_call x1, Pallas kernels: 58.4 us -> 50.2 us  [tail(): pl.pallas_call(tail_kernel, out_shape=(shp((depth // 16, hidden), f32), s...]
    pallas_call x1, Pallas kernels: 63.1 us -> 56.7 us  [middle(): pl.pallas_call(middle_kernel, out_shape=(shp((rows, wide), bf16), shp((wi...]
    pallas_call x1, Pallas kernels: 71.7 us -> 67.5 us  [head(): pl.pallas_call(head_kernel, out_shape=(shp((rows, hidden), bf16), shp((ro...]
where the time goes in v4:
time: 178 us
  Pallas kernels  177 us (99%)
    pallas_call x1, Pallas kernels, head(): pl.pallas_call(head_kernel, out_shape=(shp((rows, hidden), bf16), shp((ro...  67.5 us
    pallas_call x1, Pallas kernels, middle(): pl.pallas_call(middle_kernel, out_shape=(shp((rows, wide), bf16), shp((wi...  56.7 us
    pallas_call x1, Pallas kernels, tail(): pl.pallas_call(tail_kernel, out_shape=(shp((depth // 16, hidden), f32), s...  50.2 us

profile of v4, /device:TPU:1, one launch (start us, length us, event | category | flops | bytes accessed | tf_op | source)
XLA Modules:
  0.0 178.1 jit_solution(3692595742887300385)
XLA Ops:
  0.6 67.5 %head.1 = (bf16[512,1024]{1,0:T(8,128)(2,1)}, f32[512,1024]{1,0:T(8,128)}, bf16[512,384]{1,0:T(8,128)(2,1)}, f32[64,384]{1,0:T(8,128)}, f32[64,128]{1,0:T(8,128)...) custom-call(bf16[512,4096]{1,0:T(8,128)(2,1)} %tokens.3, bf16[256,1024]{1,0:T(8,128)(2,1)} %w_in.1, ...), custom_call_target="tpu_custom_call" | custom-call | tf_op jit(solution)/shard_map/head/pallas_call | solution.py:433
  68.2 56.7 %middle.1 = (bf16[512,384]{1,0:T(8,128)(2,1)}, f32[24,6144]{1,0:T(8,128)}, f32[8,512]{1,0:T(8,128)}) custom-call(bf16[512,384]{1,0:T(8,128)(2,1)} %get-tuple-element.23.sn, bf16[384,6144]{1,0:T(8,128)(2,1)} %proto_s.1, bf16[512,6144]{1,0:T(8,128)(2,1)} %get-tuple-element.24.et_in, f32[8,512]{1,0:T(8,128)} %get-tuple-element.25.stat_t, s32[1,512]{1,0:T(1,128)} %bitcast.4, ...), custom_call_target="tpu_custom_call" | custom-call | tf_op jit(solution)/shard_map/middle/pallas_call | solution.py:664
  124.9 50.2 %tail.1 = (f32[256,1024]{1,0:T(8,128)}, bf16[1024,384]{1,0:T(8,128)(2,1)}, f32[8,128]{1,0:T(8,128)}) custom-call(bf16[512,4096]{1,0:T(8,128)(2,1)} %tokens.3, bf16[512,1024]{1,0:T(8,128)(2,1)} %get-tuple-element.21.hid_in, f32[512,1024]{1,0:T(8,128)} %get-tuple-element.22.slope_in, bf16[512,384]{1,0:T(8,128)(2,1)} %get-tuple-element.28.dbott, ...), custom_call_target="tpu_custom_call" | custom-call | tf_op jit(solution)/shard_map/tail/pallas_call | solution.py:811
  175.0 3.1 %close.1 = (f32[256,1024]{1,0:T(8,128)}, f32[1024,384]{1,0:T(8,128)}, f32[24,6144]{1,0:T(8,128)}, f32[1,1]{1,0:T(1,128)}) custom-call(f32[256,1024]{1,0:T(8,128)} %get-tuple-element.30.wg, bf16[1024,384]{1,0:T(8,128)(2,1)} %get-tuple-element.31.wo, f32[24,6144]{1,0:T(8,128)} %get-tuple-element.32.pg, f32[8,128]{1,0:T(8,128)} %get-tuple-element.33.loss), custom_call_target="tpu_custom_call" | custom-call | tf_op jit(solution)/shard_map/close/pallas_call | solution.py:848

commit v5 on v4

--- a/solution.py
+++ b/solution.py
@@ -162,6 +162,21 @@
     yield [(cxf, at.chip(True, 2))]
 
 
+def gather_small(cps, at, buf):
+    xl = at.p % 2
+    other = at.p + 1 - 2 * xl
+    ring = [(at.r, (at.p + 2 * k) % 8) for k in (1, 2, 3)]
+    over = cps.start(buf.at[at.p], buf.at[at.p], (at.r, other))
+    first = [cps.start(buf.at[at.p], buf.at[at.p], dev) for dev in ring]
+    yield
+    over.wait_recv()
+    second = [cps.start(buf.at[other], buf.at[other], dev) for dev in ring]
+    yield
+    for k in first + second:
+        k.wait_recv()
+    yield
+
+
 def across(row):
     return jnp.transpose(jnp.broadcast_to(row, (128, row.shape[1])))
 
@@ -297,12 +312,9 @@
         gather_rows(cps, at, w_in, wbuf, 128, 128, 64, 64, 32),
     ]
 
-    def advance():
-        return list(zip(*[next(g) for g in halves]))
-
-    def accumulate(landed):
+    def accumulate(*landed):
         block = wbuf.shape[1] * 2
-        for (one, chip), (two, _) in landed:
+        for (one, chip), (two, _) in zip(*landed):
             one.wait_recv()
             two.wait_recv()
             lhs = tok[:, pl.ds(pl.multiple_of(chip * block, block), block)]
@@ -315,12 +327,14 @@
 
             lax.fori_loop(0, pre.shape[1] // 256, tile, 0)
 
-    tc = [cps.start(tbuf.at[at.p], tbuf.at[at.p], at.proto_peer(d)) for d in range(1, 8)]
-    started = advance()
+    teach = gather_small(cps, at, tbuf)
+    next(teach)
+    a0, b0 = (next(g) for g in halves)
     pre[...] = jnp.zeros_like(pre)
     load_pt.wait()
-    for k in tc:
-        k.wait_recv()
+    next(teach)
+    a1 = next(halves[0])
+    next(teach)
     tn = tbuf[...].reshape(rows, tbuf.shape[2])
     step = 512
 
@@ -334,9 +348,7 @@
         return best
 
     top[...] = lax.fori_loop(0, kk // step, score, jnp.full((rows, 128), -jnp.inf, f32))
-    own.wait()
-    load_tok.wait()
-    first = advance()
+    b1 = next(halves[1])
     top[...] = jnp.broadcast_to(jnp.max(top[...], axis=1, keepdims=True), (rows, 128))
 
     def lift(i, _):
@@ -344,21 +356,29 @@
         peak = top[rs, :]
 
         def tile(j, acc):
-            for q in range(4):
-                cols = pl.ds(pl.multiple_of(j * 512 + q * 128, 128), 128)
+            for q in range(8):
+                cols = pl.ds(pl.multiple_of(j * 1024 + q * 128, 128), 128)
                 e = jnp.exp(lt[rs, cols] - peak)
                 et[rs, cols] = e.astype(bf16)
                 acc = acc + e
             return acc
 
-        tot[rs, :] = lax.fori_loop(0, kk // 512, tile, jnp.zeros((64, 128), f32))
+        tot[rs, :] = lax.fori_loop(0, kk // 1024, tile, jnp.zeros((64, 128), f32))
         return 0
 
-    lax.fori_loop(0, rows // 64, lift, 0)
+    lax.fori_loop(0, rows // 128, lift, 0)
+    own.wait()
+    load_tok.wait()
+    a2 = next(halves[0])
+    lax.fori_loop(rows // 128, rows // 64, lift, 0)
     save = pltpu.make_async_copy(et, et_o, lsem.at[3])
     save.start()
-    accumulate(started)
-    second = advance()
+    b2 = next(halves[1])
+    accumulate(a0, b0)
+    accumulate(a1, b1)
+    a3 = next(halves[0])
+    accumulate(a2, b2)
+    b3 = next(halves[1])
     stat_o[...] = jnp.concatenate(
         [
             jnp.transpose(top[...])[0:1],
@@ -367,10 +387,7 @@
         ],
         axis=0,
     )
-    accumulate(first)
-    accumulate(second)
-    third = advance()
-    accumulate(third)
+    accumulate(a3, b3)
 
     small = part.shape[1]
 
@@ -462,7 +479,7 @@
 def middle_kernel(
     sn, proto_s, et_in, stat_t, image, unit, recip,
     dbott_o, pgrad_o, loss_o,
-    ps, et, ls, gs, snt, ms, ss, cs, cbuf, stats, fsb, ftb,
+    ps, et, ls, gs, gs_, snt, ms, ss, cs, cbuf, stats, fsb, ftb,
     S, snd, rc, far, nm, np_, xb, xa, fin, fcore,
     S_, snd_, rc_, far_, nm_, np__, xb_, xa_, fin_, fcore_,
     dacc, dpart, drecv, dbuf, send, recv, lsem,
@@ -473,15 +490,21 @@
     half = kk // 2
     peers = [at.proto_peer(d) for d in range(1, 8)] + [at.row_peer(d) for d in range(1, 16)]
     greet(peers)
-    load_ps = pltpu.make_async_copy(proto_s, ps, lsem.at[0])
-    load_ps.start()
+    third = kk // 3
+    load_ps = [
+        pltpu.make_async_copy(
+            proto_s.at[:, pl.ds(i * third, third)], ps.at[:, pl.ds(i * third, third)], lsem.at[2 + i]
+        )
+        for i in range(3)
+    ]
+    for k in load_ps:
+        k.start()
     load_et = pltpu.make_async_copy(et_in, et, lsem.at[1])
     load_et.start()
     snt[...] = jnp.transpose(sn[...])
     images = cbuf.shape[1]
     onehot = (lax.broadcasted_iota(jnp.int32, (images, rows), 0) == image[...]).astype(f32)
     cbuf[at.r] = jnp.broadcast_to(jnp.sum(onehot, axis=1, keepdims=True), cbuf.shape[1:])
-    load_ps.wait()
     step = 512
 
     def one(j, top):
@@ -492,7 +515,10 @@
             top = jnp.maximum(top, v[:, q * 128 : (q + 1) * 128])
         return top
 
-    ms[...] = lax.fori_loop(0, kk // step, one, jnp.full((rows, 128), -jnp.inf, f32))
+    ms[...] = jnp.full((rows, 128), -jnp.inf, f32)
+    for i in range(3):
+        load_ps[i].wait()
+        ms[...] = lax.fori_loop(i * third // step, (i + 1) * third // step, one, ms[...])
     met(len(peers))
     cc = [cps.start(cbuf.at[at.r], cbuf.at[at.r], at.row_peer(d)) for d in range(1, 16)]
     ms[...] = jnp.broadcast_to(jnp.max(ms[...], axis=1, keepdims=True), (rows, 128))
@@ -504,8 +530,8 @@
 
         def tile(j, acc):
             s, c = acc
-            for q in range(4):
-                cols = pl.ds(pl.multiple_of(j * 512 + q * 128, 128), 128)
+            for q in range(8):
+                cols = pl.ds(pl.multiple_of(j * 1024 + q * 128, 128), 128)
                 d = ls[rs, cols] - peak
                 e = jnp.exp(d)
                 ls[rs, cols] = e
@@ -514,7 +540,7 @@
             return s, c
 
         zero = jnp.zeros((64, 128), f32)
-        ss[rs, :], cs[rs, :] = lax.fori_loop(0, kk // 512, tile, (zero, zero))
+        ss[rs, :], cs[rs, :] = lax.fori_loop(0, kk // 1024, tile, (zero, zero))
         return 0
 
     lax.fori_loop(0, rows // 64, two, 0)
@@ -555,36 +581,40 @@
     ftb[...] = across(lift * jnp.exp(mine[0:1] - top_t) / total_t)
     dacc[...] = jnp.zeros_like(dacc)
 
-    def grads(base, dst):
-        def one(j, _):
-            first = base + j * step
-
-            def block(i, _):
-                rs = pl.ds(pl.multiple_of(i * 64, 64), 64)
-                f_s, f_t = fsb[rs, :], ftb[rs, :]
-                for q in range(step // 128):
-                    cols = pl.ds(pl.multiple_of(first + q * 128, 128), 128)
-                    v = ls[rs, cols] * f_s - et[rs, cols].astype(f32) * f_t
-                    gs[rs, q * 128 : (q + 1) * 128] = v.astype(bf16)
-                return 0
-
-            lax.fori_loop(0, rows // 64, block, 0)
-            cols = pl.ds(pl.multiple_of(first, step), step)
-            g = gs[...]
+    mine_at, other_at = at.c * half, (1 - at.c) * half
+    quarter = half // 2
+    firsts = [
+        base + where + j * step
+        for where in (0, quarter)
+        for base in (other_at, mine_at)
+        for j in range(quarter // step)
+    ]
+
+    def fill(t):
+        dst = (gs, gs_)[t % 2]
+        for i in range(0, rows, 64):
+            f_s, f_t = fsb[i : i + 64, :], ftb[i : i + 64, :]
+            for q in range(step // 128):
+                cols = pl.ds(pl.multiple_of(firsts[t] + q * 128, 128), 128)
+                v = ls[i : i + 64, cols] * f_s - et[i : i + 64, cols].astype(f32) * f_t
+                dst[i : i + 64, q * 128 : (q + 1) * 128] = v.astype(bf16)
+
+    def grads(segment, dst):
+        count = quarter // step
+        for j in range(count):
+            t = segment * count + j
+            g = (gs, gs_)[t % 2][...]
             v = jnp.dot(snt[...], g, preferred_element_type=f32)
-            dst[:, :, pl.ds(pl.multiple_of(j * step, step), step)] = v.astype(bf16).reshape(
+            dst[:, :, j * step : (j + 1) * step] = v.astype(bf16).reshape(
                 dst.shape[0], dst.shape[1], step
             )
-            d = lax.dot_general(
+            cols = pl.ds(pl.multiple_of(firsts[t], step), step)
+            dacc[...] += lax.dot_general(
                 g, ps[:, cols], (((1,), (1,)), ((), ())), preferred_element_type=f32
             )
-            dacc[...] += d
-            return 0
-
-        lax.fori_loop(0, dst.shape[2] // step, one, 0)
-
-    quarter = half // 2
-    mine_at, other_at = at.c * half, (1 - at.c) * half
+            if t + 1 < len(firsts):
+                fill(t + 1)
+
     one = Scatter(cps, at, S, (far, nm, np_, xb, xa), 1, 896, 384, 256)
     two = Scatter(cps, at, S_, (far_, nm_, np__, xb_, xa_), 1, 896, 512, 384)
 
@@ -597,13 +627,14 @@
             if other:
                 rs.ready_x(dy)
 
-    grads(other_at, snd)
+    fill(0)
+    grads(0, snd)
     swap = cps.start(snd, rc, at.CO)
-    grads(mine_at, S)
-    grads(other_at + quarter, snd_)
+    grads(1, S)
+    grads(2, snd_)
     swap_ = cps.start(snd_, rc_, at.CO)
     merge(one, S, rc, swap)
-    grads(mine_at + quarter, S_)
+    grads(3, S_)
     dpart[...] = dacc[...].astype(bf16).reshape(dpart.shape)
     dc = [
         cps.start(dpart.at[(at.p + d) % 8], drecv.at[d], at.proto_peer(d)) for d in range(1, 8)
@@ -667,12 +698,12 @@
         in_specs=[vspec(), aspec(), aspec()] + [vspec()] * 4,
         out_specs=(vspec(),) * 3,
         scratch_shapes=[
-            VMEM((wide, kk), bf16), VMEM((rows, kk), bf16), VMEM((rows, kk), f32), VMEM((rows, 512), bf16),
+            VMEM((wide, kk), bf16), VMEM((rows, kk), bf16), VMEM((rows, kk), f32), VMEM((rows, 512), bf16), VMEM((rows, 512), bf16),
             VMEM((wide, rows), bf16), lane, lane, lane, VMEM((16, 64, 128), f32), VMEM((8, 8, rows), f32), lane, lane,
             *(part + part),
             VMEM((rows, wide), f32), VMEM((8, small, wide), bf16), VMEM((8, small, wide), bf16), VMEM((8, small, wide), bf16),
             pltpu.SemaphoreType.DMA((copies,)), pltpu.SemaphoreType.DMA((copies,)),
-            pltpu.SemaphoreType.DMA((2,)),
+            pltpu.SemaphoreType.DMA((5,)),
         ],
         compiler_params=pltpu.CompilerParams(
             collective_id=1, has_side_effects=True, vmem_limit_bytes=62 * 2**20

time: 178 us -> 174 us (0.978)
  Pallas kernels: 177 us -> 174 us
    pallas_call x1, Pallas kernels: 56.7 us -> 54.3 us  [middle(): pl.pallas_call(middle_kernel, out_shape=(shp((rows, wide), bf16), shp((wi...]
where the time goes in v5:
time: 174 us
  Pallas kernels  174 us (100%)
    pallas_call x1, Pallas kernels, head(): pl.pallas_call(head_kernel, out_shape=(shp((rows, hidden), bf16), shp((ro...  67.1 us
    pallas_call x1, Pallas kernels, middle(): pl.pallas_call(middle_kernel, out_shape=(shp((rows, wide), bf16), shp((wi...  54.3 us
    pallas_call x1, Pallas kernels, tail(): pl.pallas_call(tail_kernel, out_shape=(shp((depth // 16, hidden), f32), s...  49 us

profile of v5, /device:TPU:1, one launch (start us, length us, event | category | flops | bytes accessed | tf_op | source)
XLA Modules:
  0.0 174.2 jit_solution(1214475477229380533)
XLA Ops:
  0.6 67.1 %head.1 = (bf16[512,1024]{1,0:T(8,128)(2,1)}, f32[512,1024]{1,0:T(8,128)}, bf16[512,384]{1,0:T(8,128)(2,1)}, f32[64,384]{1,0:T(8,128)}, f32[64,128]{1,0:T(8,128)...) custom-call(bf16[512,4096]{1,0:T(8,128)(2,1)} %tokens.3, bf16[256,1024]{1,0:T(8,128)(2,1)} %w_in.1, ...), custom_call_target="tpu_custom_call" | custom-call | tf_op jit(solution)/shard_map/head/pallas_call | solution.py:450
  67.8 54.3 %middle.1 = (bf16[512,384]{1,0:T(8,128)(2,1)}, f32[24,6144]{1,0:T(8,128)}, f32[8,512]{1,0:T(8,128)}) custom-call(bf16[512,384]{1,0:T(8,128)(2,1)} %get-tuple-element.23.sn, bf16[384,6144]{1,0:T(8,128)(2,1)} %proto_s.1, bf16[512,6144]{1,0:T(8,128)(2,1)} %get-tuple-element.24.et_in, f32[8,512]{1,0:T(8,128)} %get-tuple-element.25.stat_t, s32[1,512]{1,0:T(1,128)} %bitcast.4, ...), custom_call_target="tpu_custom_call" | custom-call | tf_op jit(solution)/shard_map/middle/pallas_call | solution.py:695
  122.0 49.0 %tail.1 = (f32[256,1024]{1,0:T(8,128)}, bf16[1024,384]{1,0:T(8,128)(2,1)}, f32[8,128]{1,0:T(8,128)}) custom-call(bf16[512,4096]{1,0:T(8,128)(2,1)} %tokens.3, bf16[512,1024]{1,0:T(8,128)(2,1)} %get-tuple-element.21.hid_in, f32[512,1024]{1,0:T(8,128)} %get-tuple-element.22.slope_in, bf16[512,384]{1,0:T(8,128)(2,1)} %get-tuple-element.28.dbott, ...), custom_call_target="tpu_custom_call" | custom-call | tf_op jit(solution)/shard_map/tail/pallas_call | solution.py:842
  171.1 3.1 %close.1 = (f32[256,1024]{1,0:T(8,128)}, f32[1024,384]{1,0:T(8,128)}, f32[24,6144]{1,0:T(8,128)}, f32[1,1]{1,0:T(1,128)}) custom-call(f32[256,1024]{1,0:T(8,128)} %get-tuple-element.30.wg, bf16[1024,384]{1,0:T(8,128)(2,1)} %get-tuple-element.31.wo, f32[24,6144]{1,0:T(8,128)} %get-tuple-element.32.pg, f32[8,128]{1,0:T(8,128)} %get-tuple-element.33.loss), custom_call_target="tpu_custom_call" | custom-call | tf_op jit(solution)/shard_map/close/pallas_call | solution.py:879

commit v6 on v5

--- a/solution.py
+++ b/solution.py
@@ -66,7 +66,7 @@
 
 class Copies:
     def __init__(self, send, recv):
-        self.send, self.recv, self.all = send, recv, []
+        self.send, self.recv, self.all, self.sent = send, recv, [], []
 
     def start(self, src, dst, dev):
         i = len(self.all)
@@ -94,9 +94,14 @@
         self.all.append(cp)
         return cp
 
+    def drained(self, cp):
+        cp.wait_send()
+        self.sent.append(cp)
+
     def finish(self):
         for cp in self.all:
-            cp.wait_send()
+            if not any(cp is k for k in self.sent):
+                cp.wait_send()
 
 
 def greet(peers):
@@ -476,13 +481,15 @@
     return jnp.transpose(col)
 
 
-def middle_kernel(
-    sn, proto_s, et_in, stat_t, image, unit, recip,
-    dbott_o, pgrad_o, loss_o,
-    ps, et, ls, gs, gs_, snt, ms, ss, cs, cbuf, stats, fsb, ftb,
+def rear_kernel(
+    sn, proto_s, et_in, stat_t, image, unit, recip, tokens, hid_in, slope_in, w_out,
+    pgrad_o, wgrad_o, wout_o, loss_o,
+    ps, et, ls, gs, gs_, snt, ms, ss, cs, cbuf, stats,
     S, snd, rc, far, nm, np_, xb, xa, fin, fcore,
     S_, snd_, rc_, far_, nm_, np__, xb_, xa_, fin_, fcore_,
-    dacc, dpart, drecv, dbuf, send, recv, lsem,
+    dacc, dpart, drecv, dbuf, dbott,
+    hid, dp, wS, wrc, wfar, wnm, wnp, wxb, wxa, wfcore,
+    W, S2, rc2, r2, own2, wbuf, lbuf, send, recv, lsem,
 ):
     at = Place()
     cps = Copies(send, recv)
@@ -499,8 +506,10 @@
     ]
     for k in load_ps:
         k.start()
-    load_et = pltpu.make_async_copy(et_in, et, lsem.at[1])
+    load_et = pltpu.make_async_copy(et_in, et, lsem.at[6])
     load_et.start()
+    load_hid = pltpu.make_async_copy(hid_in, hid, lsem.at[0])
+    load_hid.start()
     snt[...] = jnp.transpose(sn[...])
     images = cbuf.shape[1]
     onehot = (lax.broadcasted_iota(jnp.int32, (images, rows), 0) == image[...]).astype(f32)
@@ -574,11 +583,12 @@
         total_s = total_s + q[3:4] * jnp.exp(q[2:3] - top_s)
         cross = cross + scale * (q[4:5] + q[1:2] * (q[2:3] - top_s))
     cross = jnp.log(total_s) - cross / total_t
-    loss_o[...] = jnp.broadcast_to(w_row * cross, loss_o.shape)
+    lbuf[at.r] = jnp.broadcast_to(jnp.sum(w_row * cross, axis=1, keepdims=True), lbuf.shape[1:])
+    lc = [cps.start(lbuf.at[at.r], lbuf.at[at.r], at.row_peer(d)) for d in range(1, 16)]
     mine = stats[at.p]
     lift = (loss_scale / tau_student) * w_row
-    fsb[...] = across(lift * jnp.exp(mine[2:3] - top_s) / total_s)
-    ftb[...] = across(lift * jnp.exp(mine[0:1] - top_t) / total_t)
+    ss[...] = across(lift * jnp.exp(mine[2:3] - top_s) / total_s)
+    cs[...] = across(lift * jnp.exp(mine[0:1] - top_t) / total_t)
     dacc[...] = jnp.zeros_like(dacc)
 
     mine_at, other_at = at.c * half, (1 - at.c) * half
@@ -593,7 +603,7 @@
     def fill(t):
         dst = (gs, gs_)[t % 2]
         for i in range(0, rows, 64):
-            f_s, f_t = fsb[i : i + 64, :], ftb[i : i + 64, :]
+            f_s, f_t = ss[i : i + 64, :], cs[i : i + 64, :]
             for q in range(step // 128):
                 cols = pl.ds(pl.multiple_of(firsts[t] + q * 128, 128), 128)
                 v = ls[i : i + 64, cols] * f_s - et[i : i + 64, cols].astype(f32) * f_t
@@ -618,7 +628,7 @@
     one = Scatter(cps, at, S, (far, nm, np_, xb, xa), 1, 896, 384, 256)
     two = Scatter(cps, at, S_, (far_, nm_, np__, xb_, xa_), 1, 896, 512, 384)
 
-    def merge(rs, S, rc, swap):
+    def merge_pg(rs, S, rc, swap):
         swap.wait_recv()
         for other, dy in ORDER:
             g = at.chip(other, dy)
@@ -633,14 +643,19 @@
     grads(1, S)
     grads(2, snd_)
     swap_ = cps.start(snd_, rc_, at.CO)
-    merge(one, S, rc, swap)
+    merge_pg(one, S, rc, swap)
     grads(3, S_)
+    load_tok = pltpu.make_async_copy(tokens, et.at[:, pl.ds(0, tokens.shape[1])], lsem.at[1])
+    load_tok.start()
+    hidden = dp.shape[1]
+    load_slope = pltpu.make_async_copy(slope_in, ls.at[:, pl.ds(0, hidden)], lsem.at[5])
+    load_slope.start()
     dpart[...] = dacc[...].astype(bf16).reshape(dpart.shape)
     dc = [
         cps.start(dpart.at[(at.p + d) % 8], drecv.at[d], at.proto_peer(d)) for d in range(1, 8)
     ]
     one.mid_a(1)
-    merge(two, S_, rc_, swap_)
+    merge_pg(two, S_, rc_, swap_)
     one.mid_b(2)
     one.mid_a(0)
     total = dpart[at.p].astype(f32)
@@ -650,90 +665,16 @@
     u, r = unit[...], recip[:, 0:1]
     dbuf[at.p] = (r * (total - u * jnp.sum(u * total, axis=1, keepdims=True))).astype(bf16)
     bc = [cps.start(dbuf.at[at.p], dbuf.at[at.p], at.proto_peer(d)) for d in range(1, 8)]
+    load_hid.wait()
     one.mid_b(1)
     one.late_a()
     one.mid_b(3)
     two.mid_a(1)
     one.late_b()
     two.mid_b(2)
-    two.mid_a(0)
-    two.mid_b(1)
-    two.late_a()
-    two.mid_b(3)
-    two.late_b()
-    n = fcore.shape[0]
-    keep, give = pl.ds(pl.multiple_of(at.c * n, 8), n), pl.ds(pl.multiple_of((1 - at.c) * n, 8), n)
-
-    def settle(rs, fin, fcore, where):
-        rs.final(fin)
-        fc = cps.start(fin.at[give], fcore, at.CO)
-        pgrad_o[:, pl.ds(pl.multiple_of(mine_at + where, quarter), quarter)] = fin[keep, :]
-        return fc
-
-    fc = settle(one, fin, fcore, 0)
     for k in bc:
         k.wait_recv()
-    dbott_o[...] = dbuf[...].reshape(dbott_o.shape)
-    fc_ = settle(two, fin_, fcore_, quarter)
-    fc.wait_recv()
-    pgrad_o[:, pl.ds(pl.multiple_of(other_at, half), quarter)] = fcore[...]
-    fc_.wait_recv()
-    pgrad_o[:, pl.ds(pl.multiple_of(other_at + quarter, quarter), quarter)] = fcore_[...]
-    cps.finish()
-
-
-def middle(sn, proto_s, et, stat_t, image, unit, recip):
-    rows, wide = sn.shape
-    kk = proto_s.shape[1]
-    small = unit.shape[0]
-    shp = jax.ShapeDtypeStruct
-    chunk = (wide // 8, kk // 4)
-    copies = 15 + 7 + 7 + 7 + 2 * (1 + 23 + 1)
-    lane = VMEM((rows, 128), f32)
-    part = [VMEM((8,) + chunk, bf16)] * 3 + scatter_bufs(chunk)
-    part += [VMEM(chunk, f32), VMEM((chunk[0] // 2, chunk[1]), f32)]
-    return pl.pallas_call(
-        middle_kernel,
-        out_shape=(shp((rows, wide), bf16), shp((wide // 16, kk), f32), shp((8, rows), f32)),
-        in_specs=[vspec(), aspec(), aspec()] + [vspec()] * 4,
-        out_specs=(vspec(),) * 3,
-        scratch_shapes=[
-            VMEM((wide, kk), bf16), VMEM((rows, kk), bf16), VMEM((rows, kk), f32), VMEM((rows, 512), bf16), VMEM((rows, 512), bf16),
-            VMEM((wide, rows), bf16), lane, lane, lane, VMEM((16, 64, 128), f32), VMEM((8, 8, rows), f32), lane, lane,
-            *(part + part),
-            VMEM((rows, wide), f32), VMEM((8, small, wide), bf16), VMEM((8, small, wide), bf16), VMEM((8, small, wide), bf16),
-            pltpu.SemaphoreType.DMA((copies,)), pltpu.SemaphoreType.DMA((copies,)),
-            pltpu.SemaphoreType.DMA((5,)),
-        ],
-        compiler_params=pltpu.CompilerParams(
-            collective_id=1, has_side_effects=True, vmem_limit_bytes=62 * 2**20
-        ),
-        name="middle",
-    )(sn, proto_s, et, stat_t, image, unit, recip)
-
-
-def tail_kernel(
-    tokens, hid_in, slope_in, dbott, w_out, loss_in,
-    wgrad_o, wout_o, loss_o,
-    tok, hid, slope, dp, S, snd, rc, far, nm, np_, xb, xa, fin, fcore,
-    W, S2, rc2, r2, own2, wbuf, lbuf, send, recv, lsem,
-):
-    at = Place()
-    cps = Copies(send, recv)
-    rows, hidden = dp.shape
-    half = hidden // 2
-    peers = [at.row_peer(d) for d in range(1, 16)]
-    greet(peers)
-    load_tok = pltpu.make_async_copy(tokens, tok, lsem.at[0])
-    load_tok.start()
-    load_hid = pltpu.make_async_copy(hid_in, hid, lsem.at[2])
-    load_hid.start()
-    load_slope = pltpu.make_async_copy(slope_in, slope, lsem.at[1])
-    load_slope.start()
-    lbuf[at.r] = jnp.broadcast_to(
-        jnp.sum(loss_in[...], axis=1, keepdims=True), lbuf.shape[1:]
-    )
-    load_hid.wait()
+    dbott[...] = dbuf[...].reshape(dbott.shape)
     small = W.shape[2]
     for j in range(hidden // 256):
         cols = slice(j * 256, (j + 1) * 256)
@@ -743,9 +684,8 @@
         for i in range(256 // small):
             k = j * (256 // small) + i
             W[k % 2, k // 2] = v[i * small : (i + 1) * small]
-    met(len(peers))
     swap2 = cps.start(W.at[1 - at.c], rc2, at.CO)
-    lc = [cps.start(lbuf.at[at.r], lbuf.at[at.r], at.row_peer(d)) for d in range(1, 16)]
+    two.mid_a(0)
     load_slope.wait()
 
     def back(j, _):
@@ -753,33 +693,11 @@
         v = lax.dot_general(
             dbott[...], w_out[cols, :], (((1,), (1,)), ((), ())), preferred_element_type=f32
         )
-        dp[:, cols] = (v * slope[:, cols]).astype(bf16)
+        dp[:, cols] = (v * ls[:, cols]).astype(bf16)
         return 0
 
     lax.fori_loop(0, hidden // 256, back, 0)
-    load_tok.wait()
-    rs = Scatter(cps, at, S, (far, nm, np_, xb, xa), 0, 288, 128, 112)
-    swaps = {}
-
-    def chunk(other, dy):
-        g = at.chip(other, dy)
-        lhs = pl.ds(pl.multiple_of(g * 512, 512), 512)
-        for dst, side in ((snd, 1 - at.c), (S, at.c)):
-            rhs = pl.ds(pl.multiple_of(side * half, half), half)
-            dst[g] = lax.dot_general(
-                tok[:, lhs], dp[:, rhs], (((0,), (0,)), ((), ())), preferred_element_type=f32
-            ).astype(bf16)
-            if dst is snd:
-                swaps[other, dy] = cps.start(snd.at[g], rc.at[g], at.CO)
-
-    def merge(other, dy):
-        g = at.chip(other, dy)
-        swaps[other, dy].wait_recv()
-        S[g] = (S[g].astype(f32) + rc[g].astype(f32)).astype(bf16)
-        rs.ready(other, dy)
-        if other:
-            rs.ready_x(dy)
-
+    two.mid_b(1)
     swap2.wait_recv()
     S2[...] = (W[at.c].astype(f32) + rc2[...].astype(f32)).astype(bf16)
     around = [k for k in ORDER if k != (False, 0)]
@@ -787,11 +705,45 @@
         cps.start(S2.at[at.chip(o, dy)], r2.at[k], at.dev(at.slot(o, dy)))
         for k, (o, dy) in enumerate(around)
     ]
-    spread = []
-    for i, key in enumerate(ORDER):
-        chunk(*key)
-        if i > 0:
-            merge(*ORDER[i - 1])
+    load_tok.wait()
+    rs = Scatter(cps, at, wS, (wfar, wnm, wnp, wxb, wxa), 0, 288, 128, 112)
+    swaps = {}
+    side = hidden // 2
+
+    def chunk(i):
+        other, dy = ORDER[i]
+        g = at.chip(other, dy)
+        lhs = pl.ds(pl.multiple_of(g * 512, 512), 512)
+
+        def product(core):
+            rhs = pl.ds(pl.multiple_of(core * side, side), side)
+            return lax.dot_general(
+                et[:, lhs], dp[:, rhs], (((0,), (0,)), ((), ())), preferred_element_type=f32
+            ).astype(bf16)
+
+        slot = et.at[:, pl.ds(tokens.shape[1] + (i % 4) * 512, 512)]
+        if i >= 4:
+            cps.drained(swaps[i - 4])
+        slot[...] = product(1 - at.c)
+        swaps[i] = cps.start(slot, wrc.at[g], at.CO)
+        wS[g] = product(at.c)
+
+    def merge(i):
+        other, dy = ORDER[i]
+        g = at.chip(other, dy)
+        swaps[i].wait_recv()
+        wS[g] = (wS[g].astype(f32) + wrc[g].astype(f32)).astype(bf16)
+        rs.ready(other, dy)
+        if other:
+            rs.ready_x(dy)
+
+    chunk(0)
+    two.late_a()
+    two.mid_b(3)
+    two.late_b()
+    for i in range(1, 8):
+        chunk(i)
+        merge(i - 1)
         if i == 4:
             total = S2[at.chip(False, 0)].astype(f32)
             for k, cp in enumerate(sums):
@@ -806,9 +758,20 @@
         if i == 6:
             rs.mid_a(1)
     rs.mid_b(2)
-    merge(*ORDER[-1])
+    merge(7)
+    n = fcore.shape[0]
+    keep, give = pl.ds(pl.multiple_of(at.c * n, 8), n), pl.ds(pl.multiple_of((1 - at.c) * n, 8), n)
+
+    def settle(rs, fin, fcore, where):
+        rs.final(fin)
+        fc = cps.start(fin.at[give], fcore, at.CO)
+        pgrad_o[:, pl.ds(pl.multiple_of(mine_at + where, quarter), quarter)] = fin[keep, :]
+        return fc
+
+    fc = settle(one, fin, fcore, 0)
     rs.mid_a(0)
     rs.mid_b(1)
+    fc_ = settle(two, fin_, fcore_, quarter)
     rs.late_a()
     rs.mid_b(3)
     landed = [spread[-1]]
@@ -816,49 +779,72 @@
         cp.wait_recv()
         ref = wbuf.at[at.slot(o, (4 - dy) % 4)]
         landed.append(cps.start(ref, ref, at.CO))
+    fc.wait_recv()
+    pgrad_o[:, pl.ds(pl.multiple_of(other_at, half), quarter)] = fcore[...]
+    fc_.wait_recv()
+    pgrad_o[:, pl.ds(pl.multiple_of(other_at + quarter, quarter), quarter)] = fcore_[...]
+    for k in lc:
+        k.wait_recv()
+    loss_o[...] = jnp.sum(lbuf[...], axis=0)
     rs.late_b()
-    rs.final(fin)
-    n = fcore.shape[0]
-    fc = cps.start(fin.at[pl.ds(pl.multiple_of((1 - at.c) * n, n), n)], fcore, at.CO)
-    wgrad_o[:, pl.ds(pl.multiple_of(at.c * half, half), half)] = fin[pl.ds(pl.multiple_of(at.c * n, n), n), :]
+    wfin = ls.at[:, pl.ds(2 * hidden, side)]
+    rs.final(wfin)
+    n = wfcore.shape[0]
+    wfc = cps.start(wfin.at[pl.ds(pl.multiple_of((1 - at.c) * n, n), n)], wfcore, at.CO)
+    wgrad_o[:, pl.ds(pl.multiple_of(at.c * side, side), side)] = ls[
+        pl.ds(pl.multiple_of(at.c * n, n), n), 2 * hidden : 2 * hidden + side
+    ]
     for copy in landed:
         copy.wait_recv()
     wout_o[...] = wbuf[...].reshape(wout_o.shape)
-    for k in lc:
-        k.wait_recv()
-    loss_o[...] = jnp.sum(lbuf[...], axis=0)
-    fc.wait_recv()
-    wgrad_o[:, pl.ds(pl.multiple_of((1 - at.c) * half, half), half)] = fcore[...]
+    wfc.wait_recv()
+    wgrad_o[:, pl.ds(pl.multiple_of((1 - at.c) * side, side), side)] = wfcore[...]
     cps.finish()
 
 
-def tail(tokens, hid, slope, dbott, w_out, loss_row):
-    rows, depth = tokens.shape
-    hidden, wide = w_out.shape
+def rear(sn, proto_s, et, stat_t, image, unit, recip, tokens, hid, slope, w_out):
+    rows, wide = sn.shape
+    kk = proto_s.shape[1]
+    small = unit.shape[0]
+    depth = tokens.shape[1]
+    hidden = w_out.shape[0]
     shp = jax.ShapeDtypeStruct
+    chunk = (wide // 8, kk // 4)
     block = (depth // 8, hidden // 2)
-    small = (hidden // 16, wide)
-    copies = 15 + 1 + 8 + 23 + 7 + 8 + 7 + 1
+    slab = (hidden // 16, wide)
+    copies = 15 + 7 + 7 + 7 + 2 * (1 + 23 + 1) + 15 + 1 + 8 + 23 + 7 + 8 + 7 + 1
+    lane = VMEM((rows, 128), f32)
+    part = [VMEM((8,) + chunk, bf16)] * 3 + scatter_bufs(chunk)
+    part += [VMEM(chunk, f32), VMEM((chunk[0] // 2, chunk[1]), f32)]
+    row_block = VMEM((8, small, wide), bf16)
     return pl.pallas_call(
-        tail_kernel,
-        out_shape=(shp((depth // 16, hidden), f32), shp((hidden, wide), bf16), shp((8, 128), f32)),
-        in_specs=[aspec(), aspec(), aspec(), vspec(), vspec(), vspec()],
-        out_specs=(vspec(),) * 3,
+        rear_kernel,
+        out_shape=(
+            shp((wide // 16, kk), f32), shp((depth // 16, hidden), f32), shp((hidden, wide), bf16),
+            shp((8, 128), f32),
+        ),
+        in_specs=[vspec(), aspec(), aspec()] + [vspec()] * 4 + [aspec()] * 3 + [vspec()],
+        out_specs=(vspec(),) * 4,
         scratch_shapes=[
-            VMEM((rows, depth), bf16), VMEM((rows, hidden), bf16), VMEM((rows, hidden), f32), VMEM((rows, hidden), bf16),
-            VMEM((8,) + block, bf16), VMEM((8,) + block, bf16), VMEM((8,) + block, bf16),
-            *scatter_bufs(block), VMEM(block, f32), VMEM((block[0] // 2, block[1]), f32),
-            VMEM((2, 8) + small, bf16), VMEM((8,) + small, bf16), VMEM((8,) + small, bf16),
-            VMEM((7,) + small, bf16), VMEM(small, bf16), VMEM((16,) + small, bf16),
+            VMEM((wide, kk), bf16), VMEM((rows, kk), bf16), VMEM((rows, kk), f32),
+            VMEM((rows, 512), bf16), VMEM((rows, 512), bf16), VMEM((wide, rows), bf16),
+            lane, lane, lane, VMEM((16, 64, 128), f32), VMEM((8, 8, rows), f32),
+            *(part + part),
+            VMEM((rows, wide), f32), row_block, row_block, row_block, VMEM((rows, wide), bf16),
+            VMEM((rows, hidden), bf16), VMEM((rows, hidden), bf16),
+            VMEM((8,) + block, bf16), VMEM((8,) + block, bf16), *scatter_bufs(block),
+            VMEM((block[0] // 2, block[1]), f32),
+            VMEM((2, 8) + slab, bf16), VMEM((8,) + slab, bf16), VMEM((8,) + slab, bf16),
+            VMEM((7,) + slab, bf16), VMEM(slab, bf16), VMEM((16,) + slab, bf16),
             VMEM((16, 8, 128), f32),
             pltpu.SemaphoreType.DMA((copies,)), pltpu.SemaphoreType.DMA((copies,)),
-            pltpu.SemaphoreType.DMA((3,)),
+            pltpu.SemaphoreType.DMA((7,)),
         ],
         compiler_params=pltpu.CompilerParams(
-            collective_id=2, has_side_effects=True, vmem_limit_bytes=62 * 2**20
+            collective_id=1, has_side_effects=True, vmem_limit_bytes=67043328
         ),
-        name="tail",
-    )(tokens, hid, slope, dbott, w_out, loss_row)
+        name="rear",
+    )(sn, proto_s, et, stat_t, image, unit, recip, tokens, hid, slope, w_out)
 
 
 def close_kernel(wg, wo, pg, loss, wg_o, wo_o, pg_o, loss_o):
@@ -890,10 +876,10 @@
     hidden, slope, student_n, unit, recip, exp_t, stat_t = head(
         tokens, w_in, w_out, teacher_z, proto_teacher, center
     )
-    dbott, proto_grad, loss_row = middle(
-        student_n, proto_student, exp_t, stat_t, image_of[None, :], unit, recip
+    proto_grad, w_in_grad, w_out_grad, loss = rear(
+        student_n, proto_student, exp_t, stat_t, image_of[None, :], unit, recip,
+        tokens, hidden, slope, w_out,
     )
-    w_in_grad, w_out_grad, loss = tail(tokens, hidden, slope, dbott, w_out, loss_row)
     w_in_grad, w_out_grad, proto_grad, loss = close(w_in_grad, w_out_grad, proto_grad, loss)
     return (loss[0, 0], w_in_grad, w_out_grad, proto_grad)
 

time: 174 us -> 167 us (0.960)
  Pallas kernels: 174 us -> 166 us
    pallas_call x2 -> x1, Pallas kernels: 103 us -> 95.9 us  [rear(): pl.pallas_call(rear_kernel, out_shape=(shp((wide // 16, kk), f32), shp((d...]
where the time goes in v6:
time: 167 us
  Pallas kernels  166 us (99%)
    pallas_call x1, Pallas kernels, rear(): pl.pallas_call(rear_kernel, out_shape=(shp((wide // 16, kk), f32), shp((d...  95.9 us
    pallas_call x1, Pallas kernels, head(): pl.pallas_call(head_kernel, out_shape=(shp((rows, hidden), bf16), shp((ro...  67.1 us

profile of v6, /device:TPU:1, one launch (start us, length us, event | category | flops | bytes accessed | tf_op | source)
XLA Modules:
  0.0 166.7 jit_solution(17387696585601165553)
XLA Ops:
  0.6 67.1 %head.1 = (bf16[512,1024]{1,0:T(8,128)(2,1)}, f32[512,1024]{1,0:T(8,128)}, bf16[512,384]{1,0:T(8,128)(2,1)}, f32[64,384]{1,0:T(8,128)}, f32[64,128]{1,0:T(8,128)...) custom-call(bf16[512,4096]{1,0:T(8,128)(2,1)} %tokens.3, bf16[256,1024]{1,0:T(8,128)(2,1)} %w_in.1, ...), custom_call_target="tpu_custom_call" | custom-call | tf_op jit(solution)/shard_map/head/pallas_call | solution.py:455
  67.8 95.9 %rear.1 = (f32[24,6144]{1,0:T(8,128)}, f32[256,1024]{1,0:T(8,128)}, bf16[1024,384]{1,0:T(8,128)(2,1)}, f32[8,128]{1,0:T(8,128)}) custom-call(bf16[512,384]{1,0:T(8,128)(2,1)} %get-tuple-element.19.sn, bf16[384,6144]{1,0:T(8,128)(2,1)} %proto_s.1, bf16[512,6144]{1,0:T(8,128)(2,1)} %get-tuple-element.20.et_in, f32[8,512]{1,0:T(8,128)} %get-tuple-element.21.stat_t, ...), custom_call_target="tpu_custom_call" | custom-call | tf_op jit(solution)/shard_map/rear/pallas_call | solution.py:820
  163.7 3.0 %close.1 = (f32[256,1024]{1,0:T(8,128)}, f32[1024,384]{1,0:T(8,128)}, f32[24,6144]{1,0:T(8,128)}, f32[1,1]{1,0:T(1,128)}) custom-call(f32[256,1024]{1,0:T(8,128)} %get-tuple-element.26.wg, bf16[1024,384]{1,0:T(8,128)(2,1)} %get-tuple-element.27.wo, f32[24,6144]{1,0:T(8,128)} %get-tuple-element.28.pg, f32[8,128]{1,0:T(8,128)} %get-tuple-element.29.loss), custom_call_target="tpu_custom_call" | custom-call | tf_op jit(solution)/shard_map/close/pallas_call | solution.py:865

commit v7 on v6

--- a/solution.py
+++ b/solution.py
@@ -655,7 +655,6 @@
         cps.start(dpart.at[(at.p + d) % 8], drecv.at[d], at.proto_peer(d)) for d in range(1, 8)
     ]
     one.mid_a(1)
-    merge_pg(two, S_, rc_, swap_)
     one.mid_b(2)
     one.mid_a(0)
     total = dpart[at.p].astype(f32)
@@ -665,6 +664,7 @@
     u, r = unit[...], recip[:, 0:1]
     dbuf[at.p] = (r * (total - u * jnp.sum(u * total, axis=1, keepdims=True))).astype(bf16)
     bc = [cps.start(dbuf.at[at.p], dbuf.at[at.p], at.proto_peer(d)) for d in range(1, 8)]
+    merge_pg(two, S_, rc_, swap_)
     load_hid.wait()
     one.mid_b(1)
     one.late_a()

time: 167 us -> 165 us (0.988)
  Pallas kernels: 166 us -> 164 us
    pallas_call x1, Pallas kernels: 95.9 us -> 93.8 us  [rear(): pl.pallas_call(rear_kernel, out_shape=(shp((wide // 16, kk), f32), shp((d...]
where the time goes in v7:
time: 165 us
  Pallas kernels  164 us (99%)
    pallas_call x1, Pallas kernels, rear(): pl.pallas_call(rear_kernel, out_shape=(shp((wide // 16, kk), f32), shp((d...  93.8 us
    pallas_call x1, Pallas kernels, head(): pl.pallas_call(head_kernel, out_shape=(shp((rows, hidden), bf16), shp((ro...  67.1 us

profile of v7, /device:TPU:1, one launch (start us, length us, event | category | flops | bytes accessed | tf_op | source)
XLA Modules:
  0.0 164.6 jit_solution(2924546143681705997)
XLA Ops:
  0.6 67.1 %head.1 = (bf16[512,1024]{1,0:T(8,128)(2,1)}, f32[512,1024]{1,0:T(8,128)}, bf16[512,384]{1,0:T(8,128)(2,1)}, f32[64,384]{1,0:T(8,128)}, f32[64,128]{1,0:T(8,128)...) custom-call(bf16[512,4096]{1,0:T(8,128)(2,1)} %tokens.3, bf16[256,1024]{1,0:T(8,128)(2,1)} %w_in.1, ...), custom_call_target="tpu_custom_call" | custom-call | tf_op jit(solution)/shard_map/head/pallas_call | solution.py:455
  67.8 93.8 %rear.1 = (f32[24,6144]{1,0:T(8,128)}, f32[256,1024]{1,0:T(8,128)}, bf16[1024,384]{1,0:T(8,128)(2,1)}, f32[8,128]{1,0:T(8,128)}) custom-call(bf16[512,384]{1,0:T(8,128)(2,1)} %get-tuple-element.19.sn, bf16[384,6144]{1,0:T(8,128)(2,1)} %proto_s.1, bf16[512,6144]{1,0:T(8,128)(2,1)} %get-tuple-element.20.et_in, f32[8,512]{1,0:T(8,128)} %get-tuple-element.21.stat_t, ...), custom_call_target="tpu_custom_call" | custom-call | tf_op jit(solution)/shard_map/rear/pallas_call | solution.py:820
  161.6 3.0 %close.1 = (f32[256,1024]{1,0:T(8,128)}, f32[1024,384]{1,0:T(8,128)}, f32[24,6144]{1,0:T(8,128)}, f32[1,1]{1,0:T(1,128)}) custom-call(f32[256,1024]{1,0:T(8,128)} %get-tuple-element.26.wg, bf16[1024,384]{1,0:T(8,128)(2,1)} %get-tuple-element.27.wo, f32[24,6144]{1,0:T(8,128)} %get-tuple-element.28.pg, f32[8,128]{1,0:T(8,128)} %get-tuple-element.29.loss), custom_call_target="tpu_custom_call" | custom-call | tf_op jit(solution)/shard_map/close/pallas_call | solution.py:865
